TPU v7x, 256 devices: a whole 4x4x8 slice. The times are simulated.
256 devices in a mesh: bx: 4 (over x), by: 32 (over y, z), gz: 2 (over core).
Axes of the slice: x: 4, y: 4, z: 8, core: 2. Of those that a mesh axis runs over, the one named last changes fastest.
Arguments:
- electric_start: float32 [3, 512, 64, 256], P(None, 'by', 'bx', 'gz'), may hold values from -6 to 6
- magnetic_start: float32 [3, 512, 64, 256], P(None, 'by', 'bx', 'gz'), may hold values from -6 to 6
- current_start: float32 [3, 512, 64, 256], P(None, 'by', 'bx', 'gz'), may hold values from -6 to 6
- cotangent: float32 [3, 512, 64, 256], P(None, 'by', 'bx', 'gz'), may hold values from -6 to 6
- level_set: float32 [512, 64, 256], P('by', 'bx', 'gz'), may hold values from -8 to 8
- material: int32 [512, 64, 256], P('by', 'bx', 'gz'), may hold values from 0 to 2
- source_cell: int32 [2048], P(('bx', 'by', 'gz')), may hold values from 0 to 32767
- basis: bfloat16 [65536, 64, 256], P(('bx', 'by', 'gz')), may hold values from 0 to 1
- block_owner: int32 [65536, 1], P(('bx', 'by', 'gz')), may hold values from 0 to 127; in each aligned block of 256 rows (0 to 255, 256 to 511, ...) at most 4 rows name the same one
- block_group: int32 [65536], P(('bx', 'by', 'gz')), may hold values from 0 to 127
Outputs:
- final_electric: float32 [3, 512, 64, 256], P(None, 'by', 'bx', 'gz')
- adjoint_electric: float32 [3, 512, 64, 256], P(None, 'by', 'bx', 'gz')
- coef_grad: float32 [64, 32768], P(None, ('bx', 'by', 'gz'))
Inputs may be any that keep to these rules, and one draw needn't show every extreme that they name: `material`: 0 is vacuum, 1 design dielectric, 2 silver. `source_cell`: a flat cell index within the device's own brick; a cell may be named more than once. `block_owner`: among the 256 blocks of one device no owner is named by more than 4 blocks, and in some device one owner is named by exactly 4.
All inputs are finite; a program needn't handle non-finite values.
Results may differ from a plain program's by a relative error of at most 0.0029.
Values sent between devices are 32-bit elements; how exact they have to be, the bound alone decides.
A program may use at most 64 MiB of HBM per device.

v0:
```python
import jax
import jax.numpy as jnp
from jax import lax
from jax.sharding import PartitionSpec as P

NSTEP = 2
KB = 64
GRP_DEV = 128


time_step = 0.5
drude_keep = 0.9
drude_gain = 1.0
metal_permit = 3.0
design_contrast = 5.0
source_level = 3.0
source_wave = (1.0, -0.6, 0.8, -0.4)


def passed_along(x, axis, by):
    count = lax.axis_size(axis)
    pairs = [(i, i + by) for i in range(count) if 0 <= i + by < count]
    return lax.ppermute(x, axis, pairs)


def face_y(face_cells, offset):
    return passed_along(face_cells, "by", offset)


def face_x(face_cells, offset):
    return passed_along(face_cells, "bx", offset)


def face_z(face_cells, offset):
    return passed_along(face_cells, "gz", offset)


def beside(couple, axis_dim, offset):
    length = couple.shape[axis_dim]
    border_at = 0 if offset < 0 else length - 1
    face_cells = lax.index_in_dim(couple, border_at, axis=axis_dim, keepdims=False)
    if axis_dim == 1:
        arrived = face_y(face_cells, offset)
    elif axis_dim == 2:
        arrived = face_x(face_cells, offset)
    else:
        flattened = face_cells.reshape(face_cells.shape[0], -1)
        arrived = face_z(flattened, offset).reshape(face_cells.shape)
    arrived = jnp.expand_dims(arrived, axis_dim)
    if offset < 0:
        return jnp.concatenate(
            [lax.slice_in_dim(couple, 1, length, axis=axis_dim), arrived], axis=axis_dim
        )
    return jnp.concatenate(
        [arrived, lax.slice_in_dim(couple, 0, length - 1, axis=axis_dim)], axis=axis_dim
    )


def differ(couple, axis_dim, offset):
    neighbour = beside(couple, axis_dim, offset)
    if offset < 0:
        return neighbour - couple
    return couple - neighbour


def curl(fields, offset):
    along_x = differ(jnp.stack([fields[1], fields[2]]), 2, offset)
    along_y = differ(jnp.stack([fields[0], fields[2]]), 1, offset)
    along_z = differ(jnp.stack([fields[0], fields[1]]), 3, offset)
    return jnp.stack([along_y[1] - along_z[1], along_z[0] - along_x[1], along_x[0] - along_y[0]])


def local(
    electric_start,
    magnetic_start,
    current_start,
    cotangent,
    level_set,
    material,
    source_cell,
    basis,
    block_owner,
    block_group,
):
    silver = (material == 2).astype(jnp.float32)
    design = (material == 1).astype(jnp.float32)
    smooth = jax.nn.sigmoid(level_set)
    permit = jnp.where(
        material == 2, metal_permit, jnp.where(material == 1, 1.0 + design_contrast * smooth, 1.0)
    )
    sources = (
        jnp.zeros((material.size,), jnp.float32).at[source_cell].add(1.0).reshape(material.shape)
    )
    electric, magnetic, current = (electric_start, magnetic_start, current_start)
    drives = []
    for moment in range(NSTEP):
        magnetic = magnetic - time_step * curl(electric, -1)
        current = silver * (drude_keep * current + drude_gain * electric)
        drive_term = curl(magnetic, 1) - current
        electric = electric + time_step / permit * drive_term
        electric = electric.at[2].add(source_level * source_wave[moment] * sources)
        drives.append(drive_term)
    step_ratio = time_step / permit
    adj_electric = cotangent
    adj_magnetic = jnp.zeros_like(cotangent)
    adj_current = jnp.zeros_like(cotangent)
    eps_grad = jnp.zeros(material.shape, jnp.float32)
    for moment in reversed(range(NSTEP)):
        scaled = step_ratio * adj_electric
        eps_grad = eps_grad - jnp.sum(scaled * drives[moment], axis=0) / permit
        adj_drive = adj_current - scaled
        adj_magnetic = adj_magnetic + curl(scaled, -1)
        adj_electric = (
            adj_electric + drude_gain * silver * adj_drive - time_step * curl(adj_magnetic, 1)
        )
        adj_current = drude_keep * silver * adj_drive
    level_grad = eps_grad * design * design_contrast * (smooth * (1.0 - smooth))
    cell_grad = level_grad.astype(jnp.bfloat16)
    tile_width = basis.shape[2]
    tile_count = cell_grad.size // tile_width
    block_count = basis.shape[0]
    tile_fan = block_count // tile_count
    cell_tiles = cell_grad.reshape(tile_count, tile_width)
    blocks = basis.reshape(tile_count, tile_fan, KB, tile_width)
    partials = jnp.einsum(
        "tfkc,tc->tfk", blocks, cell_tiles, preferred_element_type=jnp.float32
    ).reshape(block_count, KB)
    size_bx = lax.axis_size("bx")
    planes = size_bx * lax.axis_size("by")
    capacity = max(2, 2 * block_count // planes)
    slots = planes * capacity
    owner_plane = block_owner[:, 0]
    owner_hits = (owner_plane[:, None] == jnp.arange(planes, dtype=jnp.int32)[None, :]).astype(
        jnp.float32
    )
    before = jnp.cumsum(owner_hits, axis=0) - owner_hits
    slot_rank = jnp.sum(before * owner_hits, axis=1).astype(jnp.int32)
    target = owner_plane * capacity + slot_rank
    placing = (target[:, None] == jnp.arange(slots, dtype=jnp.int32)[None, :]).astype(jnp.float32)
    send_vals = jnp.einsum("bk,bs->ks", partials, placing, precision=lax.Precision.HIGHEST)
    send_ids = (
        jnp.einsum(
            "b,bs->s",
            block_group.astype(jnp.float32) + 1.0,
            placing,
            precision=lax.Precision.HIGHEST,
        )[None, :]
        - 1.0
    )
    got_vals, got_ids = (
        lax.all_to_all(send_vals, ("bx", "by"), split_axis=1, concat_axis=1, tiled=True),
        lax.all_to_all(send_ids, ("bx", "by"), split_axis=1, concat_axis=1, tiled=True),
    )
    group_hits = (
        got_ids[0][:, None] == jnp.arange(GRP_DEV, dtype=jnp.int32)[None, :].astype(jnp.float32)
    ).astype(jnp.float32)
    coef_grad = jnp.dot(got_vals, group_hits, precision=lax.Precision.HIGHEST)
    return (electric, adj_electric, coef_grad)


def solution(mesh):
    return jax.shard_map(
        local,
        mesh=mesh,
        in_specs=(
            P(None, "by", "bx", "gz"),
            P(None, "by", "bx", "gz"),
            P(None, "by", "bx", "gz"),
            P(None, "by", "bx", "gz"),
            P("by", "bx", "gz"),
            P("by", "bx", "gz"),
            P(("bx", "by", "gz")),
            P(("bx", "by", "gz"), None, None),
            P(("bx", "by", "gz"), None),
            P(("bx", "by", "gz")),
        ),
        out_specs=(
            P(None, "by", "bx", "gz"),
            P(None, "by", "bx", "gz"),
            P(None, ("bx", "by", "gz")),
        ),
        check_vma=False,
    )
```

profile of v0, /device:TPU:8, one launch (start us, length us, event | category | flops | bytes accessed | tf_op | source)
XLA Modules:
  0.0 175.3 jit_solution(5927105462938856978)
XLA Ops:
  1.7 7.7 %collective-permute-start = (f32[2,16,128]{2,1,0:T(8,128)S(1)}, f32[2,16,128]{2,1,0:T(8,128)S(1)}, u32[]{:S(2)}, u32[]{:S(2)}) collective-permute-start(f32[2,16,128]{2,1,0:T(8,128)S(1)} %fusion.57), channel_id=1, source_target_pairs={{2,0},{4,2},{6,4},{8,6},{10,8},{12,10},{14,12},{16,14},{18,16},{20... | collective-permute-start | bytes 49160 | tf_op jit(solution)/shard_map/ppermute | solution.py:23
  9.4 1.1 slice_reduce_fusion.6
  10.6 1.4 collective-permute-start.1
  12.9 1.3 collective-permute-start.2
  18.6 11.3 %all-to-all-start.1 = ((f32[1,128,4]{2,0,1:T(1,128)}), f32[1,128,4]{2,0,1:T(1,128)S(1)}, u32[]{:S(2)}, u32[]{:S(2)}) async-start(f32[1,128,4]{2,0,1:T(1,128)} %bitcast.57), calls=%async_computation.1 | async-start | bytes 131072 | tf_op jit(solution)/shard_map/all_to_all | solution.py:152
  30.6 1.6 broadcast_select_fusion
  34.2 1.6 fusion.42
  36.4 1.1 slice.463
  38.7 2.5 %all-to-all-done.1 = f32[1,128,4]{2,0,1:T(1,128)S(1)} async-done(((f32[1,128,4]{2,0,1:T(1,128)}), f32[1,128,4]{2,0,1:T(1,128)S(1)}, u32[]{:S(2)}, u32[]{:S(2)}) %all-to-all-start.1) | async-done | bytes 2080 | tf_op jit(solution)/shard_map/all_to_all | solution.py:152
  43.2 1.2 maximum_subtract_fusion.2
  47.7 2.6 %collective-permute-start.3 = (f32[2,16,128]{2,1,0:T(8,128)}, f32[2,16,128]{2,1,0:T(8,128)S(1)}, u32[]{:S(2)}, u32[]{:S(2)}) collective-permute-start(f32[2,16,128]{2,1,0:T(8,128)} %fusion.58), channel_id=1, source_target_pairs={{0,2},{2,4},{4,6},{6,8},{8,10},{10,12},{12,14},{14,16},{16,18},{18... | collective-permute-start | bytes 49160 | tf_op jit(solution)/shard_map/ppermute | solution.py:23
  50.4 1.9 %collective-permute-start.4 = (f32[2,256]{1,0:T(2,128)S(1)}, f32[2,256]{1,0:T(2,128)}, u32[]{:S(2)}, u32[]{:S(2)}) collective-permute-start(f32[2,256]{1,0:T(2,128)S(1)} %reshape_squeeze.25), channel_id=1, source_target_pairs={{0,1},{2,3},{4,5},{6,7},{8,9},{10,11},{12,13},{14,15},{16,17},{18,... | collective-permute-start | bytes 6152 | tf_op jit(solution)/shard_map/ppermute | solution.py:23
  52.9 2.4 %collective-permute-start.5 = (f32[2,16,128]{2,1,0:T(8,128)}, f32[2,16,128]{2,1,0:T(8,128)S(1)}, u32[]{:S(2)}, u32[]{:S(2)}) collective-permute-start(f32[2,16,128]{2,1,0:T(8,128)} %bitcast.8), channel_id=1, source_target_pairs={{0,64},{64,128},{128,192},{1,65},{65,129},{129,193},{2,66},{66,130... | collective-permute-start | bytes 49160 | tf_op jit(solution)/shard_map/ppermute | solution.py:23
  59.4 5.1 %collective-permute-start.6 = (f32[2,16,128]{2,1,0:T(8,128)S(1)}, f32[2,16,128]{2,1,0:T(8,128)S(1)}, u32[]{:S(2)}, u32[]{:S(2)}) collective-permute-start(f32[2,16,128]{2,1,0:T(8,128)S(1)} %fusion.59), channel_id=1, source_target_pairs={{2,0},{4,2},{6,4},{8,6},{10,8},{12,10},{14,12},{16,14},{18,16},{20... | collective-permute-start | bytes 49160 | tf_op jit(solution)/shard_map/ppermute | solution.py:23
  64.6 1.3 collective-permute-start.7
  66.0 1.3 collective-permute-start.13
  72.3 1.3 collective-permute-start.8
  73.6 1.9 %collective-permute-start.12 = (f32[2,16,128]{2,1,0:T(8,128)}, f32[2,16,128]{2,1,0:T(8,128)}, u32[]{:S(2)}, u32[]{:S(2)}) collective-permute-start(f32[2,16,128]{2,1,0:T(8,128)} %fusion.61), channel_id=1, source_target_pairs={{2,0},{4,2},{6,4},{8,6},{10,8},{12,10},{14,12},{16,14},{18,16},{20... | collective-permute-start | bytes 49160 | tf_op jit(solution)/shard_map/ppermute | solution.py:23
  75.5 1.3 collective-permute-start.14
  79.7 1.3 slice_subtract_fusion.9
  81.0 1.1 fusion.4
  84.1 1.3 slice_subtract_fusion.5
  87.2 3.9 %collective-permute-start.9 = (f32[2,16,128]{2,1,0:T(8,128)S(1)}, f32[2,16,128]{2,1,0:T(8,128)S(1)}, u32[]{:S(2)}, u32[]{:S(2)}) collective-permute-start(f32[2,16,128]{2,1,0:T(8,128)S(1)} %fusion.60), channel_id=1, source_target_pairs={{0,2},{2,4},{4,6},{6,8},{8,10},{10,12},{12,14},{14,16},{16,18},{18... | collective-permute-start | bytes 49160 | tf_op jit(solution)/shard_map/ppermute | solution.py:23
  91.2 2.5 %collective-permute-start.10 = (f32[2,256]{1,0:T(2,128)S(1)}, f32[2,256]{1,0:T(2,128)S(1)}, u32[]{:S(2)}, u32[]{:S(2)}) collective-permute-start(f32[2,256]{1,0:T(2,128)S(1)} %reshape_squeeze.27), channel_id=1, source_target_pairs={{0,1},{2,3},{4,5},{6,7},{8,9},{10,11},{12,13},{14,15},{16,17},{18,... | collective-permute-start | bytes 6152 | tf_op jit(solution)/shard_map/ppermute | solution.py:23
  93.7 1.3 collective-permute-start.16
  96.5 5.5 %collective-permute-start.11 = (f32[2,16,128]{2,1,0:T(8,128)S(1)}, f32[2,16,128]{2,1,0:T(8,128)S(1)}, u32[]{:S(2)}, u32[]{:S(2)}) collective-permute-start(f32[2,16,128]{2,1,0:T(8,128)S(1)} %bitcast.137), channel_id=1, source_target_pairs={{0,64},{64,128},{128,192},{1,65},{65,129},{129,193},{2,66},{66,130... | collective-permute-start | bytes 49160 | tf_op jit(solution)/shard_map/ppermute | solution.py:23
  101.9 3.6 %collective-permute-start.17 = (f32[2,16,128]{2,1,0:T(8,128)S(1)}, f32[2,16,128]{2,1,0:T(8,128)S(1)}, u32[]{:S(2)}, u32[]{:S(2)}) collective-permute-start(f32[2,16,128]{2,1,0:T(8,128)S(1)} %bitcast.129), channel_id=1, source_target_pairs={{0,64},{64,128},{128,192},{1,65},{65,129},{129,193},{2,66},{66,130... | collective-permute-start | bytes 49160 | tf_op jit(solution)/shard_map/ppermute | solution.py:23
  105.6 2.2 %collective-permute-start.15 = (f32[2,16,128]{2,1,0:T(8,128)S(1)}, f32[2,16,128]{2,1,0:T(8,128)S(1)}, u32[]{:S(2)}, u32[]{:S(2)}) collective-permute-start(f32[2,16,128]{2,1,0:T(8,128)S(1)} %fusion.56), channel_id=1, source_target_pairs={{0,2},{2,4},{4,6},{6,8},{8,10},{10,12},{12,14},{14,16},{16,18},{18... | collective-permute-start | bytes 49160 | tf_op jit(solution)/shard_map/ppermute | solution.py:23
  110.6 1.3 slice_subtract_fusion.7
  111.9 1.4 collective-permute-done.15
  113.3 1.2 fusion.18
  114.7 1.3 multiply_reduce_fusion.1
  117.9 4.4 %collective-permute-start.18 = (f32[2,16,128]{2,1,0:T(8,128)}, f32[2,16,128]{2,1,0:T(8,128)S(1)}, u32[]{:S(2)}, u32[]{:S(2)}) collective-permute-start(f32[2,16,128]{2,1,0:T(8,128)} %fusion.62), channel_id=1, source_target_pairs={{2,0},{4,2},{6,4},{8,6},{10,8},{12,10},{14,12},{16,14},{18,16},{20... | collective-permute-start | bytes 49160 | tf_op jit(solution)/shard_map/ppermute | solution.py:23
  122.9 1.5 collective-permute-start.19
  124.4 6.7 %fusion.70 = f32[128,1,2,64]{3,1,2,0:T(1,128)S(1)} fusion(bf16[128,256,1,1]{1,2,3,0:T(2,128)(2,1)S(1)} %reshape.178, bf16[128,2,64,256]{3,2,1,0:T(8,128)(2,1)} %bitcast.110), kind=kOutput, calls=%fused_computation.204 | convolution fusion | flops 8388608 | bytes 8519680 | tf_op jit(solution)/shard_map/tfkc,tc->tfk/dot_general | solution.py:125
  131.1 1.2 fusion
  134.7 1.9 %reshape.198 = f32[128,1,256]{2,1,0:T(1,128)} reshape(f32[128,4,64]{2,1,0:T(4,128)} %bitcast.112) | data formatting | bytes 262144
  136.5 10.4 %all-to-all-start = ((f32[128,1,256]{2,1,0:T(1,128)}), f32[128,1,256]{2,1,0:T(1,128)}, u32[]{:S(2)}, u32[]{:S(2)}) async-start(f32[128,1,256]{2,1,0:T(1,128)} %reshape.198), calls=%async_computation | async-start | bytes 262144 | tf_op jit(solution)/shard_map/all_to_all | solution.py:151
  146.9 1.3 collective-permute-start.20
  148.2 1.6 broadcast_in_dim_reshape.38
  150.8 2.3 %collective-permute-done.20 = f32[2,16,128]{2,1,0:T(8,128)S(1)} collective-permute-done((f32[2,16,128]{2,1,0:T(8,128)}, f32[2,16,128]{2,1,0:T(8,128)S(1)}, u32[]{:S(2)}, u32[]{:S(2)}) %collective-permute-start.20) | collective-permute-done | bytes 16416 | tf_op jit(solution)/shard_map/ppermute | solution.py:23
  153.1 1.1 slice_subtract_fusion.3
  155.9 3.3 %collective-permute-start.21 = (f32[2,16,128]{2,1,0:T(8,128)}, f32[2,16,128]{2,1,0:T(8,128)S(1)}, u32[]{:S(2)}, u32[]{:S(2)}) collective-permute-start(f32[2,16,128]{2,1,0:T(8,128)} %fusion.63), channel_id=1, source_target_pairs={{0,2},{2,4},{4,6},{6,8},{8,10},{10,12},{12,14},{14,16},{16,18},{18... | collective-permute-start | bytes 49160 | tf_op jit(solution)/shard_map/ppermute | solution.py:23
  159.3 2.4 %collective-permute-start.22 = (f32[2,256]{1,0:T(2,128)S(1)}, f32[2,256]{1,0:T(2,128)}, u32[]{:S(2)}, u32[]{:S(2)}) collective-permute-start(f32[2,256]{1,0:T(2,128)S(1)} %reshape_squeeze.31), channel_id=1, source_target_pairs={{0,1},{2,3},{4,5},{6,7},{8,9},{10,11},{12,13},{14,15},{16,17},{18,... | collective-permute-start | bytes 6152 | tf_op jit(solution)/shard_map/ppermute | solution.py:23
  162.4 3.6 %collective-permute-start.23 = (f32[2,16,128]{2,1,0:T(8,128)}, f32[2,16,128]{2,1,0:T(8,128)S(1)}, u32[]{:S(2)}, u32[]{:S(2)}) collective-permute-start(f32[2,16,128]{2,1,0:T(8,128)} %bitcast.40), channel_id=1, source_target_pairs={{0,64},{64,128},{128,192},{1,65},{65,129},{129,193},{2,66},{66,130... | collective-permute-start | bytes 49160 | tf_op jit(solution)/shard_map/ppermute | solution.py:23
  168.1 1.9 %fusion.6 = (f32[3,16,16,128]{3,2,1,0:T(8,128)}, f32[3,16,16,128]{3,2,1,0:T(8,128)S(1)}) fusion(f32[1,16,16,128]{3,2,1,0:T(8,128)S(1)} %get-tuple-element.64, f32[1,16,16,128]{3,2,1,0:T(8,128)S(1)} %get-tuple-element.65, f32[1,16,16,128]{3,2,1,0:T(8,128)S(1)} %get-tuple-element.63, f32[16,16,128]{2,1,0:T(8,128)} %get-tuple-element.30, ...), kind=kLoop, calls=%fused_computation.26 | loop fusion | flops 1867776 | bytes 3145728 | tf_op jit(solution)/shard_map/sub | solution.py:114
  171.5 1.9 %reduce.24 = f32[128,256]{1,0:T(8,128)S(1)} reduce(f32[128,1,256]{2,1,0:T(1,128)} %all-to-all-done, f32[]{:T(128)} %broadcast.190), dimensions={1}, to_apply=%all_to_all.12.reduce_sub_computation | reduce | bytes 262148 | tf_op jit(solution)/shard_map/all_to_all | solution.py:151
  173.5 1.8 fusion.24
  (172 shorter events, 49.1 us)
Async XLA Ops:
  0.6 45.2 %copy-start.2 = (f32[3,16,16,128]{3,2,1,0:T(8,128)S(1)}, f32[3,16,16,128]{3,2,1,0:T(8,128)}, u32[]{:S(2)}) copy-start(f32[3,16,16,128]{3,2,1,0:T(8,128)} %param.15) | copy-start | bytes 1179652
  1.7 41.5 %collective-permute-start = (f32[2,16,128]{2,1,0:T(8,128)S(1)}, f32[2,16,128]{2,1,0:T(8,128)S(1)}, u32[]{:S(2)}, u32[]{:S(2)}) collective-permute-start(f32[2,16,128]{2,1,0:T(8,128)S(1)} %fusion.57), channel_id=1, source_target_pairs={{2,0},{4,2},{6,4},{8,6},{10,8},{12,10},{14,12},{16,14},{18,16},{20... | collective-permute-start | bytes 49160 | tf_op jit(solution)/shard_map/ppermute | solution.py:23
  10.4 46.8 %copy-start = (f32[3,16,16,128]{3,2,1,0:T(8,128)S(1)}, f32[3,16,16,128]{3,2,1,0:T(8,128)}, u32[]{:S(2)}) copy-start(f32[3,16,16,128]{3,2,1,0:T(8,128)} %param.14) | copy-start | bytes 1179652
  10.5 46.8 %copy-start.1 = (f32[3,16,16,128]{3,2,1,0:T(8,128)S(1)}, f32[3,16,16,128]{3,2,1,0:T(8,128)}, u32[]{:S(2)}) copy-start(f32[3,16,16,128]{3,2,1,0:T(8,128)} %param.17) | copy-start | bytes 1179652
  10.5 46.8 %copy-start.3 = (f32[3,16,16,128]{3,2,1,0:T(8,128)S(1)}, f32[3,16,16,128]{3,2,1,0:T(8,128)}, u32[]{:S(2)}) copy-start(f32[3,16,16,128]{3,2,1,0:T(8,128)} %param.16) | copy-start | bytes 1179652
  10.6 27.9 %collective-permute-start.1 = (f32[2,256]{1,0:T(2,128)S(1)}, f32[2,256]{1,0:T(2,128)S(1)}, u32[]{:S(2)}, u32[]{:S(2)}) collective-permute-start(f32[2,256]{1,0:T(2,128)S(1)} %reshape_squeeze.24), channel_id=1, source_target_pairs={{1,0},{3,2},{5,4},{7,6},{9,8},{11,10},{13,12},{15,14},{17,16},{19,... | collective-permute-start | bytes 6152 | tf_op jit(solution)/shard_map/ppermute | solution.py:23
  12.9 30.3 %collective-permute-start.2 = (f32[2,16,128]{2,1,0:T(8,128)S(1)}, f32[2,16,128]{2,1,0:T(8,128)S(1)}, u32[]{:S(2)}, u32[]{:S(2)}) collective-permute-start(f32[2,16,128]{2,1,0:T(8,128)S(1)} %bitcast.135), channel_id=1, source_target_pairs={{64,0},{128,64},{192,128},{65,1},{129,65},{193,129},{66,2},{130,66... | collective-permute-start | bytes 49160 | tf_op jit(solution)/shard_map/ppermute | solution.py:23
  16.9 1.0 copy-start.14
  18.6 22.5 %all-to-all-start.1 = ((f32[1,128,4]{2,0,1:T(1,128)}), f32[1,128,4]{2,0,1:T(1,128)S(1)}, u32[]{:S(2)}, u32[]{:S(2)}) async-start(f32[1,128,4]{2,0,1:T(1,128)} %bitcast.57), calls=%async_computation.1 | async-start | bytes 131072 | tf_op jit(solution)/shard_map/all_to_all | solution.py:152
  32.2 6.3 %copy-start.13 = (pred[16,16,128]{2,1,0:T(8,128)(4,1)}, pred[16,16,128]{2,1,0:T(8,128)(4,1)S(1)}, u32[]{:S(2)}) copy-start(pred[16,16,128]{2,1,0:T(8,128)(4,1)S(1)} %get-tuple-element.31) | copy-start | bytes 98308
  45.1 0.6 copy-start.11
  47.7 8.6 %collective-permute-start.3 = (f32[2,16,128]{2,1,0:T(8,128)}, f32[2,16,128]{2,1,0:T(8,128)S(1)}, u32[]{:S(2)}, u32[]{:S(2)}) collective-permute-start(f32[2,16,128]{2,1,0:T(8,128)} %fusion.58), channel_id=1, source_target_pairs={{0,2},{2,4},{4,6},{6,8},{8,10},{10,12},{12,14},{14,16},{16,18},{18... | collective-permute-start | bytes 49160 | tf_op jit(solution)/shard_map/ppermute | solution.py:23
  50.4 5.0 %collective-permute-start.4 = (f32[2,256]{1,0:T(2,128)S(1)}, f32[2,256]{1,0:T(2,128)}, u32[]{:S(2)}, u32[]{:S(2)}) collective-permute-start(f32[2,256]{1,0:T(2,128)S(1)} %reshape_squeeze.25), channel_id=1, source_target_pairs={{0,1},{2,3},{4,5},{6,7},{8,9},{10,11},{12,13},{14,15},{16,17},{18,... | collective-permute-start | bytes 6152 | tf_op jit(solution)/shard_map/ppermute | solution.py:23
  52.9 4.1 %collective-permute-start.5 = (f32[2,16,128]{2,1,0:T(8,128)}, f32[2,16,128]{2,1,0:T(8,128)S(1)}, u32[]{:S(2)}, u32[]{:S(2)}) collective-permute-start(f32[2,16,128]{2,1,0:T(8,128)} %bitcast.8), channel_id=1, source_target_pairs={{0,64},{64,128},{128,192},{1,65},{65,129},{129,193},{2,66},{66,130... | collective-permute-start | bytes 49160 | tf_op jit(solution)/shard_map/ppermute | solution.py:23
  57.2 1.2 copy-start.4
  59.4 19.3 %collective-permute-start.6 = (f32[2,16,128]{2,1,0:T(8,128)S(1)}, f32[2,16,128]{2,1,0:T(8,128)S(1)}, u32[]{:S(2)}, u32[]{:S(2)}) collective-permute-start(f32[2,16,128]{2,1,0:T(8,128)S(1)} %fusion.59), channel_id=1, source_target_pairs={{2,0},{4,2},{6,4},{8,6},{10,8},{12,10},{14,12},{16,14},{18,16},{20... | collective-permute-start | bytes 49160 | tf_op jit(solution)/shard_map/ppermute | solution.py:23
  64.6 10.9 %collective-permute-start.7 = (f32[2,256]{1,0:T(2,128)S(1)}, f32[2,256]{1,0:T(2,128)S(1)}, u32[]{:S(2)}, u32[]{:S(2)}) collective-permute-start(f32[2,256]{1,0:T(2,128)S(1)} %reshape_squeeze.26), channel_id=1, source_target_pairs={{1,0},{3,2},{5,4},{7,6},{9,8},{11,10},{13,12},{15,14},{17,16},{19,... | collective-permute-start | bytes 6152 | tf_op jit(solution)/shard_map/ppermute | solution.py:23
  66.0 11.8 %collective-permute-start.13 = (f32[2,256]{1,0:T(2,128)S(1)}, f32[2,256]{1,0:T(2,128)S(1)}, u32[]{:S(2)}, u32[]{:S(2)}) collective-permute-start(f32[2,256]{1,0:T(2,128)S(1)} %reshape_squeeze.28), channel_id=1, source_target_pairs={{1,0},{3,2},{5,4},{7,6},{9,8},{11,10},{13,12},{15,14},{17,16},{19,... | collective-permute-start | bytes 6152 | tf_op jit(solution)/shard_map/ppermute | solution.py:23
  72.3 7.3 %collective-permute-start.8 = (f32[2,16,128]{2,1,0:T(8,128)S(1)}, f32[2,16,128]{2,1,0:T(8,128)S(1)}, u32[]{:S(2)}, u32[]{:S(2)}) collective-permute-start(f32[2,16,128]{2,1,0:T(8,128)S(1)} %bitcast.136), channel_id=1, source_target_pairs={{64,0},{128,64},{192,128},{65,1},{129,65},{193,129},{66,2},{130,66... | collective-permute-start | bytes 49160 | tf_op jit(solution)/shard_map/ppermute | solution.py:23
  73.6 9.5 %collective-permute-start.12 = (f32[2,16,128]{2,1,0:T(8,128)}, f32[2,16,128]{2,1,0:T(8,128)}, u32[]{:S(2)}, u32[]{:S(2)}) collective-permute-start(f32[2,16,128]{2,1,0:T(8,128)} %fusion.61), channel_id=1, source_target_pairs={{2,0},{4,2},{6,4},{8,6},{10,8},{12,10},{14,12},{16,14},{18,16},{20... | collective-permute-start | bytes 49160 | tf_op jit(solution)/shard_map/ppermute | solution.py:23
  75.5 8.6 %collective-permute-start.14 = (f32[2,16,128]{2,1,0:T(8,128)}, f32[2,16,128]{2,1,0:T(8,128)S(1)}, u32[]{:S(2)}, u32[]{:S(2)}) collective-permute-start(f32[2,16,128]{2,1,0:T(8,128)} %bitcast.25), channel_id=1, source_target_pairs={{64,0},{128,64},{192,128},{65,1},{129,65},{193,129},{66,2},{130,66... | collective-permute-start | bytes 49160 | tf_op jit(solution)/shard_map/ppermute | solution.py:23
  87.2 22.4 %collective-permute-start.9 = (f32[2,16,128]{2,1,0:T(8,128)S(1)}, f32[2,16,128]{2,1,0:T(8,128)S(1)}, u32[]{:S(2)}, u32[]{:S(2)}) collective-permute-start(f32[2,16,128]{2,1,0:T(8,128)S(1)} %fusion.60), channel_id=1, source_target_pairs={{0,2},{2,4},{4,6},{6,8},{8,10},{10,12},{12,14},{14,16},{16,18},{18... | collective-permute-start | bytes 49160 | tf_op jit(solution)/shard_map/ppermute | solution.py:23
  91.2 14.4 %collective-permute-start.10 = (f32[2,256]{1,0:T(2,128)S(1)}, f32[2,256]{1,0:T(2,128)S(1)}, u32[]{:S(2)}, u32[]{:S(2)}) collective-permute-start(f32[2,256]{1,0:T(2,128)S(1)} %reshape_squeeze.27), channel_id=1, source_target_pairs={{0,1},{2,3},{4,5},{6,7},{8,9},{10,11},{12,13},{14,15},{16,17},{18,... | collective-permute-start | bytes 6152 | tf_op jit(solution)/shard_map/ppermute | solution.py:23
  93.7 15.0 %collective-permute-start.16 = (f32[2,256]{1,0:T(2,128)S(1)}, f32[2,256]{1,0:T(2,128)S(1)}, u32[]{:S(2)}, u32[]{:S(2)}) collective-permute-start(f32[2,256]{1,0:T(2,128)S(1)} %reshape_squeeze.29), channel_id=1, source_target_pairs={{0,1},{2,3},{4,5},{6,7},{8,9},{10,11},{12,13},{14,15},{16,17},{18,... | collective-permute-start | bytes 6152 | tf_op jit(solution)/shard_map/ppermute | solution.py:23
  96.5 14.1 %collective-permute-start.11 = (f32[2,16,128]{2,1,0:T(8,128)S(1)}, f32[2,16,128]{2,1,0:T(8,128)S(1)}, u32[]{:S(2)}, u32[]{:S(2)}) collective-permute-start(f32[2,16,128]{2,1,0:T(8,128)S(1)} %bitcast.137), channel_id=1, source_target_pairs={{0,64},{64,128},{128,192},{1,65},{65,129},{129,193},{2,66},{66,130... | collective-permute-start | bytes 49160 | tf_op jit(solution)/shard_map/ppermute | solution.py:23
  101.9 10.0 %collective-permute-start.17 = (f32[2,16,128]{2,1,0:T(8,128)S(1)}, f32[2,16,128]{2,1,0:T(8,128)S(1)}, u32[]{:S(2)}, u32[]{:S(2)}) collective-permute-start(f32[2,16,128]{2,1,0:T(8,128)S(1)} %bitcast.129), channel_id=1, source_target_pairs={{0,64},{64,128},{128,192},{1,65},{65,129},{129,193},{2,66},{66,130... | collective-permute-start | bytes 49160 | tf_op jit(solution)/shard_map/ppermute | solution.py:23
  105.6 7.7 %collective-permute-start.15 = (f32[2,16,128]{2,1,0:T(8,128)S(1)}, f32[2,16,128]{2,1,0:T(8,128)S(1)}, u32[]{:S(2)}, u32[]{:S(2)}) collective-permute-start(f32[2,16,128]{2,1,0:T(8,128)S(1)} %fusion.56), channel_id=1, source_target_pairs={{0,2},{2,4},{4,6},{6,8},{8,10},{10,12},{12,14},{14,16},{16,18},{18... | collective-permute-start | bytes 49160 | tf_op jit(solution)/shard_map/ppermute | solution.py:23
  114.6 1.3 copy-start.5
  114.6 1.3 copy-start.7
  114.7 1.3 copy-start.9
  117.9 31.9 %collective-permute-start.18 = (f32[2,16,128]{2,1,0:T(8,128)}, f32[2,16,128]{2,1,0:T(8,128)S(1)}, u32[]{:S(2)}, u32[]{:S(2)}) collective-permute-start(f32[2,16,128]{2,1,0:T(8,128)} %fusion.62), channel_id=1, source_target_pairs={{2,0},{4,2},{6,4},{8,6},{10,8},{12,10},{14,12},{16,14},{18,16},{20... | collective-permute-start | bytes 49160 | tf_op jit(solution)/shard_map/ppermute | solution.py:23
  122.9 25.3 %collective-permute-start.19 = (f32[2,256]{1,0:T(2,128)}, f32[2,256]{1,0:T(2,128)}, u32[]{:S(2)}, u32[]{:S(2)}) collective-permute-start(f32[2,256]{1,0:T(2,128)} %reshape_squeeze.30), channel_id=1, source_target_pairs={{1,0},{3,2},{5,4},{7,6},{9,8},{11,10},{13,12},{15,14},{17,16},{19,... | collective-permute-start | bytes 6152 | tf_op jit(solution)/shard_map/ppermute | solution.py:23
  131.1 37.0 %copy-start.6 = (f32[1,16,16,128]{3,2,1,0:T(8,128)S(1)}, f32[1,16,16,128]{3,2,1,0:T(8,128)}, u32[]{:S(2)}) copy-start(f32[1,16,16,128]{3,2,1,0:T(8,128)} %copy-done.5) | copy-start | bytes 393220
  131.1 37.0 %copy-start.8 = (f32[1,16,16,128]{3,2,1,0:T(8,128)S(1)}, f32[1,16,16,128]{3,2,1,0:T(8,128)}, u32[]{:S(2)}) copy-start(f32[1,16,16,128]{3,2,1,0:T(8,128)} %copy-done.7) | copy-start | bytes 393220
  131.1 37.0 %copy-start.10 = (f32[1,16,16,128]{3,2,1,0:T(8,128)S(1)}, f32[1,16,16,128]{3,2,1,0:T(8,128)}, u32[]{:S(2)}) copy-start(f32[1,16,16,128]{3,2,1,0:T(8,128)} %copy-done.9) | copy-start | bytes 393220
  136.5 34.4 %all-to-all-start = ((f32[128,1,256]{2,1,0:T(1,128)}), f32[128,1,256]{2,1,0:T(1,128)}, u32[]{:S(2)}, u32[]{:S(2)}) async-start(f32[128,1,256]{2,1,0:T(1,128)} %reshape.198), calls=%async_computation | async-start | bytes 262144 | tf_op jit(solution)/shard_map/all_to_all | solution.py:151
  146.9 6.2 %collective-permute-start.20 = (f32[2,16,128]{2,1,0:T(8,128)}, f32[2,16,128]{2,1,0:T(8,128)S(1)}, u32[]{:S(2)}, u32[]{:S(2)}) collective-permute-start(f32[2,16,128]{2,1,0:T(8,128)} %bitcast.138), channel_id=1, source_target_pairs={{64,0},{128,64},{192,128},{65,1},{129,65},{193,129},{66,2},{130,66... | collective-permute-start | bytes 49160 | tf_op jit(solution)/shard_map/ppermute | solution.py:23
  155.9 11.0 %collective-permute-start.21 = (f32[2,16,128]{2,1,0:T(8,128)}, f32[2,16,128]{2,1,0:T(8,128)S(1)}, u32[]{:S(2)}, u32[]{:S(2)}) collective-permute-start(f32[2,16,128]{2,1,0:T(8,128)} %fusion.63), channel_id=1, source_target_pairs={{0,2},{2,4},{4,6},{6,8},{8,10},{10,12},{12,14},{14,16},{16,18},{18... | collective-permute-start | bytes 49160 | tf_op jit(solution)/shard_map/ppermute | solution.py:23
  159.3 6.7 %collective-permute-start.22 = (f32[2,256]{1,0:T(2,128)S(1)}, f32[2,256]{1,0:T(2,128)}, u32[]{:S(2)}, u32[]{:S(2)}) collective-permute-start(f32[2,256]{1,0:T(2,128)S(1)} %reshape_squeeze.31), channel_id=1, source_target_pairs={{0,1},{2,3},{4,5},{6,7},{8,9},{10,11},{12,13},{14,15},{16,17},{18,... | collective-permute-start | bytes 6152 | tf_op jit(solution)/shard_map/ppermute | solution.py:23
  162.4 5.5 %collective-permute-start.23 = (f32[2,16,128]{2,1,0:T(8,128)}, f32[2,16,128]{2,1,0:T(8,128)S(1)}, u32[]{:S(2)}, u32[]{:S(2)}) collective-permute-start(f32[2,16,128]{2,1,0:T(8,128)} %bitcast.40), channel_id=1, source_target_pairs={{0,64},{64,128},{128,192},{1,65},{65,129},{129,193},{2,66},{66,130... | collective-permute-start | bytes 49160 | tf_op jit(solution)/shard_map/ppermute | solution.py:23
  170.9 4.4 %copy-start.12 = (f32[3,16,16,128]{3,2,1,0:T(8,128)}, f32[3,16,16,128]{3,2,1,0:T(8,128)S(1)}, u32[]{:S(2)}) copy-start(f32[3,16,16,128]{3,2,1,0:T(8,128)S(1)} %fusion.37) | copy-start | bytes 1179652
where the time goes:
time: 178 us; the launch traced here: 175 us
  starting transfers between devices  86.5 us (49%)
  other arithmetic  41.9 us (24%)
  local copies, waits for them, and re-layouts  28.3 us (16%)
  matrix products  10 us (6%)
  waiting for transfers between devices  6.91 us (4%)
    ppermute x24, starting transfers between devices, passed_along(): return lax.ppermute(x, axis, pairs)  64.8 us
    all_to_all x1, starting transfers between devices, local(): lax.all_to_all(send_ids, ('bx', 'by'), split_axis=1, concat_axis=1, tiled...  11.3 us
    all_to_all x1, starting transfers between devices, local(): lax.all_to_all(send_vals, ('bx', 'by'), split_axis=1, concat_axis=1, tile...  10.4 us
    sub x8, other arithmetic, differ(): return neighbour - couple  7.75 us
    another operation x8, local copies, waits for them, and re-layouts, beside(): arrived = jnp.expand_dims(arrived, axis_dim)  7.18 us
    dot_general x1, matrix products, local(): jnp.einsum('tfkc,tc->tfk', blocks, cell_tiles, preferred_element_type=jnp...  6.71 us
    slice x8, local copies, waits for them, and re-layouts, beside(): lax.slice_in_dim(couple, 1, length, axis=axis_dim)  5.3 us
    slice x13, local copies, waits for them, and re-layouts, beside(): lax.index_in_dim(couple, border_at, axis=axis_dim, keepdims=False)  5.01 us
  transfers between devices with their start and end apart: 26, of which 4 were waited for; matrix products, arithmetic and copies ran while one was open for 34% of the time, Pallas kernels for 0%

commit v1 on v0

v1 whole, which is shorter than its diff:
```python
import jax
import jax.numpy as jnp
from jax import lax
from jax.experimental import pallas as pl
from jax.experimental.pallas import tpu as pltpu
from jax.sharding import PartitionSpec as P

KB = 64
GRP_DEV = 128
NBX = 4
NBY = 32
PLANES = 128
NB = 256
TILES = 128
TILE = 256
NCHUNK = 8

time_step = 0.5
drude_keep = 0.9
drude_gain = 1.0
metal_permit = 3.0
design_contrast = 5.0
source_level = 3.0
source_wave = (1.0, -0.6, 0.8, -0.4)

F32 = jnp.float32
BF16 = jnp.bfloat16
MESH = pl.DeviceIdType.MESH

IDX = {("x", 0): 0, ("z", 0): 1, ("x", 1): 2, ("z", 1): 3, ("y", 0): 4, ("y", 1): 5}
COMP = {"x": 0, "y": 1, "z": 2}


def iota(shape, dim):
    return lax.broadcasted_iota(jnp.int32, shape, dim)


def split(v):
    hi = v.astype(BF16)
    lo = (v - hi.astype(F32)).astype(BF16)
    return hi, lo


def kernel(
    source_ref,
    e0_hbm,
    h0_hbm,
    j0_hbm,
    cot_hbm,
    level_hbm,
    material_hbm,
    basis_hbm,
    owner_hbm,
    group_hbm,
    e_out,
    a_out,
    coef_out,
    p1,
    p2,
    m1,
    m2,
    h0,
    j0,
    cot,
    level,
    material,
    ratio,
    silver,
    factor,
    sources,
    d1,
    adj1,
    part1,
    grad,
    efin,
    afin,
    basis,
    owner,
    group,
    xsend,
    xrecv,
    zsend,
    zrecv,
    place,
    partial,
    vsend,
    vrecv,
    isend,
    irecv,
    coef,
    in_sem,
    basis_sem,
    out_sem,
    send_sem,
    recv_sem,
    a2a_sem,
    own_sem,
    ready_sem,
):
    bx, by, gz = lax.axis_index("bx"), lax.axis_index("by"), lax.axis_index("gz")
    me = bx * NBY + by
    yy, zz = by // 8, by % 8
    xy = bx * 4 + yy

    loads = [
        (material_hbm, material),
        (level_hbm, level),
        (cot_hbm, cot),
        (e0_hbm.at[0], p1.at[0, pl.ds(0, 16)]),
        (e0_hbm.at[2], p1.at[1, pl.ds(0, 16)]),
        (e0_hbm.at[1], p1.at[4, pl.ds(0, 16)]),
        (h0_hbm, h0),
        (j0_hbm, j0),
        (owner_hbm, owner),
        (group_hbm, group),
    ]
    loads = [pltpu.make_async_copy(s, d, in_sem.at[i]) for i, (s, d) in enumerate(loads)]
    for c in loads:
        c.start()

    zrow = jnp.zeros((4, 16, 128), F32)
    for ref, at in ((p1, 16), (p2, 16), (m1, 0), (m2, 0)):
        ref[0:4, at] = zrow
    for r in range(4):
        xrecv[r] = zrow
        zrecv[r] = jnp.zeros((16, 128), F32)

    barrier = pltpu.get_barrier_semaphore()

    def hail(**where):
        pl.semaphore_signal(barrier, inc=1, device_id=where, device_id_type=MESH)

    for i in range(1, 8):
        hail(by=yy * 8 + (zz + i) % 8)
    for i in range(1, 16):
        q = (xy + i) % 16
        hail(bx=q // 4, by=(q % 4) * 8 + zz)
    hail(gz=1 - gz)
    up_far = jnp.logical_and(zz == 7, by < NBY - 1)
    down_far = jnp.logical_and(zz == 0, by > 0)

    @pl.when(up_far)
    def _():
        hail(by=by + 1)

    @pl.when(down_far)
    def _():
        hail(by=by - 1)

    for c in loads[:6]:
        c.wait()
    bases = [
        pltpu.make_async_copy(
            basis_hbm.at[pl.ds(i * (NB * KB // NCHUNK), NB * KB // NCHUNK)],
            basis.at[pl.ds(i * (NB * KB // NCHUNK), NB * KB // NCHUNK)],
            basis_sem.at[i],
        )
        for i in range(NCHUNK)
    ]
    for c in bases:
        c.start()

    row = iota((16, 128), 0)
    lane = iota((16, 128), 1)

    def pack_z(acc, y, vals, from_lane):
        for c, v in enumerate(vals):
            at = 4 * y + c
            acc = jnp.where(lane == at, pltpu.roll(v, (at + 128 - from_lane) % 128, 1), acc)
        return acc

    def first(y, acc):
        mat = material[y]
        lev = level[y]
        smooth = jax.nn.sigmoid(lev)
        design = (mat == 1).astype(F32)
        sil = (mat == 2).astype(F32)
        permit = jnp.where(mat == 2, metal_permit, jnp.where(mat == 1, 1.0 + design_contrast * smooth, 1.0))
        rat = time_step / permit
        ratio[y] = rat
        silver[y] = sil
        factor[y] = -(design * design_contrast * (smooth * (1.0 - smooth))) / permit
        sx, sy, sz = (rat * cot[c, y] for c in range(3))
        p1[2, y] = sx
        p1[3, y] = sz
        p1[5, y] = sy
        ex, ey, ez = p1[0, y], p1[4, y], p1[1, y]
        for c, v in enumerate((ey, ez, sy, sz)):
            xsend[0, c, pl.ds(y, 1), :] = v[0:1]
        return pack_z(acc, y, (ex, ey, sx, sy), 0)

    zsend[0] = lax.fori_loop(0, 16, first, jnp.zeros((16, 128), F32))

    pl.semaphore_wait(barrier, 23 + up_far.astype(jnp.int32) + down_far.astype(jnp.int32))
    for i in range(1, 16):
        q = (xy + i) % 16
        pl.semaphore_signal(
            ready_sem, inc=1, device_id={"bx": q // 4, "by": (q % 4) * 8 + zz}, device_id_type=MESH
        )

    def moves(r, field):
        plus = r % 2 == 0
        step = -1 if plus else 1
        edge, halo = (0, 16) if plus else (16, 0)

        def move(src, dst, i, **where):
            return pltpu.make_async_remote_copy(
                src_ref=src,
                dst_ref=dst,
                send_sem=send_sem.at[r, i],
                recv_sem=recv_sem.at[r, i],
                device_id=where,
                device_id_type=MESH,
            )

        y_out = by > 0 if plus else by < NBY - 1
        y_in = by < NBY - 1 if plus else by > 0
        x_out = bx > 0 if plus else bx < NBX - 1
        x_in = bx < NBX - 1 if plus else bx > 0
        z_out = gz == 1 if plus else gz == 0
        z_in = gz == 0 if plus else gz == 1
        return (
            (y_out, y_in, move(field.at[pl.ds(0, 4), edge], field.at[pl.ds(0, 4), halo], 0, by=by + step)),
            (x_out, x_in, move(xsend.at[r], xrecv.at[r], 1, bx=bx + step)),
            (z_out, z_in, move(zsend.at[r], zrecv.at[r], 2, gz=1 - gz)),
        )

    def send(r, field):
        for out, _, c in moves(r, field):
            pl.when(out)(c.start)

    def receive(r, field):
        for out, into, c in moves(r, field):
            pl.when(into)(c.wait_recv)
            pl.when(out)(c.wait_send)

    send(0, p1)

    for c in loads[6:]:
        c.wait()

    def count(y, _):
        flat = y * 2048 + row * 128 + lane
        total = jnp.zeros((16, 128), F32)
        for i in range(8):
            total = total + (flat == source_ref[i]).astype(F32)
        sources[y] = total
        return 0

    lax.fori_loop(0, 16, count, 0)

    owner_row = owner[...].astype(F32)
    group_row = group[...].astype(F32)
    ri, ci = iota((NB, NB), 0), iota((NB, NB), 1)
    owner_wide = jnp.broadcast_to(owner_row, (NB, NB))
    owner_col = jnp.sum(jnp.where(ri == ci, owner_wide, 0.0), axis=1, keepdims=True)
    group_col = jnp.sum(jnp.where(ri == ci, jnp.broadcast_to(group_row, (NB, NB)), 0.0), axis=1, keepdims=True)
    same = jnp.logical_and(owner_wide == owner_col, ci < ri)
    rank_col = jnp.sum(same.astype(F32), axis=1, keepdims=True)
    target_col = owner_col * 4.0 + rank_col
    block, tile = iota((NB, TILES), 0), iota((NB, TILES), 1)
    id_sum = jnp.zeros((PLANES, 128), F32)
    dest, id_lane = iota((PLANES, TILES), 0), iota((PLANES, TILES), 1)
    targets, groups = [], []
    for f in range(2):
        pick = block == 2 * tile + f
        targets.append(jnp.sum(jnp.where(pick, target_col, 0.0), axis=0, keepdims=True))
        groups.append(jnp.sum(jnp.where(pick, group_col, 0.0), axis=0, keepdims=True))
    slot_row = (2 * iota((NB, TILES), 0)).astype(F32)
    for h in range(2):
        for f in range(2):
            place[:, pl.ds((2 * h + f) * TILES, TILES)] = (
                (targets[f] == slot_row + float(h)).astype(F32).astype(BF16)
            )
    first_slot = (4 * dest).astype(F32)
    for s in range(4):
        hit = jnp.zeros((PLANES, TILES), F32)
        for f in range(2):
            hit = hit + jnp.where(targets[f] == first_slot + float(s), groups[f], 0.0)
        id_sum = jnp.where(id_lane == s, jnp.sum(hit, axis=1, keepdims=True), id_sum)
    isend[:, 0, :] = id_sum

    def plus_half(r, field, old, out):
        nxt = r + 1

        def body(y, acc):
            zf = zrecv[r]
            vals = {}
            for s in range(2):
                fx, fy, fz = (field[IDX[(c, s)], y] for c in "xyz")
                dyx = field[IDX[("x", s)], y + 1] - fx
                dyz = field[IDX[("z", s)], y + 1] - fz

                def along_x(v, c):
                    return jnp.where(row == 15, xrecv[r, c, pl.ds(y, 1), :], pltpu.roll(v, 15, 0)) - v

                def along_z(v, c):
                    return jnp.where(lane == 127, pltpu.roll(zf, 127 - 4 * y - c, 1), pltpu.roll(v, 127, 1)) - v

                dxy, dxz = along_x(fy, 2 * s), along_x(fz, 2 * s + 1)
                dzx, dzy = along_z(fx, 2 * s), along_z(fy, 2 * s + 1)
                turn = {"x": dyz - dzy, "y": dzx - dxz, "z": dxy - dyx}
                for c in "xyz":
                    new = old(s, c, y, turn[c])
                    out[IDX[(c, s)], y + 1] = new
                    vals[(c, s)] = new
            for i, k in enumerate((("y", 0), ("z", 0), ("y", 1), ("z", 1))):
                xsend[nxt, i, pl.ds(y, 1), :] = vals[k][15:16]
            return pack_z(acc, y, [vals[k] for k in (("x", 0), ("y", 0), ("x", 1), ("y", 1))], 127)

        zsend[nxt] = lax.fori_loop(0, 16, body, jnp.zeros((16, 128), F32))

    def minus_turn(r, field, y, s):
        zf = zrecv[r]
        fx, fy, fz = (field[IDX[(c, s)], y + 1] for c in "xyz")
        dyx = fx - field[IDX[("x", s)], y]
        dyz = fz - field[IDX[("z", s)], y]

        def along_x(v, c):
            return v - jnp.where(row == 0, xrecv[r, c, pl.ds(y, 1), :], pltpu.roll(v, 1, 0))

        def along_z(v, c):
            return v - jnp.where(lane == 0, pltpu.roll(zf, 128 - 4 * y - c, 1), pltpu.roll(v, 1, 1))

        dxy, dxz = along_x(fy, 2 * s), along_x(fz, 2 * s + 1)
        dzx, dzy = along_z(fx, 2 * s), along_z(fy, 2 * s + 1)
        return {"x": dyz - dzy, "y": dzx - dxz, "z": dxy - dyx}

    def old_first(s, c, y, turn):
        return turn if s else h0[COMP[c], y] - time_step * turn

    def old_second(s, c, y, turn):
        before = m1[IDX[(c, s)], y + 1]
        return before + turn if s else before - time_step * turn

    receive(0, p1)
    plus_half(0, p1, old_first, m1)
    send(1, m1)

    pl.semaphore_wait(ready_sem, 15)

    def spread(src, dst, width, k):
        def one(i, _):
            p = (me + i) % PLANES
            pltpu.make_async_remote_copy(
                src_ref=src.at[pl.ds(p * width, width)],
                dst_ref=dst.at[pl.ds(me * width, width)],
                send_sem=a2a_sem.at[k, 0],
                recv_sem=a2a_sem.at[k, 1],
                device_id={"bx": p // NBY, "by": p % NBY},
                device_id_type=MESH,
            ).start()
            return 0

        own = pltpu.make_async_copy(
            src.at[pl.ds(me * width, width)], dst.at[pl.ds(me * width, width)], own_sem.at[k]
        )
        own.start()
        lax.fori_loop(1, PLANES, one, 0, unroll=4)

    def gathered(src, dst, width, k):
        many = pl.ds(0, (PLANES - 1) * width)
        pltpu.make_async_copy(src.at[many], src.at[many], a2a_sem.at[k, 0]).wait()
        pltpu.make_async_copy(dst.at[many], dst.at[many], a2a_sem.at[k, 1]).wait()
        pltpu.make_async_copy(
            src.at[pl.ds(me * width, width)], dst.at[pl.ds(me * width, width)], own_sem.at[k]
        ).wait()

    spread(isend, irecv, 1, 0)

    receive(1, m1)

    def electric_first(y, acc):
        rat, sil = ratio[y], silver[y]
        turn, back = minus_turn(1, m1, y, 0), minus_turn(1, m1, y, 1)
        total = jnp.zeros((16, 128), F32)
        fwd, adj = {}, {}
        for c in "xyz":
            e = p1[IDX[(c, 0)], y]
            cur = sil * (drude_keep * j0[COMP[c], y] + drude_gain * e)
            drive = turn[c] - cur
            j0[COMP[c], y] = cur
            new = e + rat * drive
            if c == "z":
                new = new + source_level * source_wave[0] * sources[y]
            fwd[c] = new
            p2[IDX[(c, 0)], y] = new
            scaled = p1[IDX[(c, 1)], y]
            a = cot[COMP[c], y] - drude_gain * (sil * scaled) - time_step * back[c]
            adj1[COMP[c], y] = a
            s0 = rat * a
            adj[c] = s0
            p2[IDX[(c, 1)], y] = s0
            total = total + s0 * drive
        part1[y] = total
        for i, v in enumerate((fwd["y"], fwd["z"], adj["y"], adj["z"])):
            xsend[2, i, pl.ds(y, 1), :] = v[0:1]
        return pack_z(acc, y, (fwd["x"], fwd["y"], adj["x"], adj["y"]), 0)

    zsend[2] = lax.fori_loop(0, 16, electric_first, jnp.zeros((16, 128), F32))
    send(2, p2)
    receive(2, p2)
    plus_half(2, p2, old_second, m2)
    send(3, m2)
    receive(3, m2)

    def electric_second(y, _):
        rat, sil = ratio[y], silver[y]
        turn, back = minus_turn(3, m2, y, 0), minus_turn(3, m2, y, 1)
        total = part1[y]
        for c in "xyz":
            e = p2[IDX[(c, 0)], y]
            cur = sil * (drude_keep * j0[COMP[c], y] + drude_gain * e)
            drive = turn[c] - cur
            new = e + rat * drive
            if c == "z":
                new = new + source_level * source_wave[1] * sources[y]
            efin[COMP[c], y] = new
            scaled = p1[IDX[(c, 1)], y]
            s0 = p2[IDX[(c, 1)], y]
            adj_drive = -drude_keep * (sil * scaled) - s0
            afin[COMP[c], y] = adj1[COMP[c], y] + drude_gain * (sil * adj_drive) - time_step * back[c]
            total = total + scaled * drive
        grad[pl.ds(pl.multiple_of(y * 16, 16), 16), :] = factor[y] * total
        return 0

    lax.fori_loop(0, 16, electric_second, 0)
    outs = [
        pltpu.make_async_copy(efin, e_out, out_sem.at[0]),
        pltpu.make_async_copy(afin, a_out, out_sem.at[1]),
    ]
    for c in outs:
        c.start()
    for c in bases:
        c.wait()

    low128 = iota((16, 128), 1) < 64
    r256, l256 = iota((16, 256), 0), iota((16, 256), 1)

    def tiles(i, _):
        start = pl.multiple_of(i * 16, 16)
        even = grad[pl.ds(2 * start, 16, stride=2), :]
        odd = grad[pl.ds(2 * start + 1, 16, stride=2), :]
        lhs = jnp.concatenate([even.astype(BF16), odd.astype(BF16)], axis=1)
        acc = jnp.zeros((16, 256), F32)
        for j in range(8):
            w = basis[pl.ds(pl.multiple_of(i * 2048 + j * 256, 256), 256), :]
            got = lax.dot_general(lhs, w, (((1,), (1,)), ((), ())), preferred_element_type=F32)
            acc = jnp.where(r256 == 2 * j + l256 // 128, got, acc)
        partial[pl.ds(start, 16), :] = jnp.where(row % 2 == 0, acc[:, :128], acc[:, 128:])
        return 0

    lax.fori_loop(0, 8, tiles, 0)

    part = partial[...]
    turned = pltpu.roll(part, 64, 1)
    low = iota((TILES, 128), 1) < 64
    stack = jnp.concatenate(
        [
            jnp.where(low, part, 0.0),
            jnp.where(low, turned, 0.0),
            jnp.where(low, 0.0, turned),
            jnp.where(low, 0.0, part),
        ],
        axis=0,
    )
    hi, lo = split(stack)
    slots = lax.dot_general(place[...], hi, (((1,), (0,)), ((), ())), preferred_element_type=F32)
    slots = slots + lax.dot_general(place[...], lo, (((1,), (0,)), ((), ())), preferred_element_type=F32)
    vsend[:, 0, :] = slots
    spread(vsend, vrecv, 2, 1)

    gathered(isend, irecv, 1, 0)
    ids = irecv[:, 0, :]
    group_lane = iota((PLANES, GRP_DEV), 1).astype(F32)
    hits = jnp.concatenate(
        [
            jnp.concatenate(
                [(ids[:, 2 * p + h : 2 * p + h + 1] == group_lane).astype(F32).astype(BF16) for h in range(2)], axis=1
            )
            for p in range(2)
        ],
        axis=0,
    )
    gathered(vsend, vrecv, 2, 1)
    vals = jnp.concatenate([vrecv[pl.ds(p, PLANES, stride=2), 0, :] for p in range(2)], axis=0)
    hi, lo = split(vals)
    both = lax.dot_general(hi, hits, (((0,), (0,)), ((), ())), preferred_element_type=F32)
    both = both + lax.dot_general(lo, hits, (((0,), (0,)), ((), ())), preferred_element_type=F32)
    coef[...] = both[:KB, :GRP_DEV] + both[KB:, GRP_DEV:]
    last = pltpu.make_async_copy(coef, coef_out, out_sem.at[2])
    last.start()
    for c in outs:
        c.wait()
    last.wait()


def local(
    electric_start,
    magnetic_start,
    current_start,
    cotangent,
    level_set,
    material,
    source_cell,
    basis,
    block_owner,
    block_group,
):
    field = (3, 16, 16, 128)
    brick = (16, 16, 128)
    anywhere = pl.BlockSpec(memory_space=pl.ANY)
    V, D = pltpu.VMEM, pltpu.SemaphoreType.DMA
    return pl.pallas_call(
        kernel,
        name="adjoint_step",
        out_shape=(
            jax.ShapeDtypeStruct(field, F32),
            jax.ShapeDtypeStruct(field, F32),
            jax.ShapeDtypeStruct((KB, GRP_DEV), F32),
        ),
        in_specs=[pl.BlockSpec(memory_space=pltpu.SMEM)] + [anywhere] * 9,
        out_specs=(anywhere,) * 3,
        scratch_shapes=[
            V((6, 17, 16, 128), F32),
            V((6, 17, 16, 128), F32),
            V((6, 17, 16, 128), F32),
            V((6, 17, 16, 128), F32),
            V(field, F32),
            V(field, F32),
            V(field, F32),
            V(brick, F32),
            V(brick, jnp.int32),
            V(brick, F32),
            V(brick, F32),
            V(brick, F32),
            V(brick, F32),
            V((8, 128), F32),
            V(field, F32),
            V(brick, F32),
            V((256, 128), F32),
            V(field, F32),
            V(field, F32),
            V((NB * KB, TILE), BF16),
            V((1, NB), jnp.int32),
            V((1, NB), jnp.int32),
            V((4, 4, 16, 128), F32),
            V((4, 4, 16, 128), F32),
            V((4, 16, 128), F32),
            V((4, 16, 128), F32),
            V((NB, 4 * TILES), BF16),
            V((TILES, 128), F32),
            V((NB, 1, 128), F32),
            V((NB, 1, 128), F32),
            V((PLANES, 1, 128), F32),
            V((PLANES, 1, 128), F32),
            V((KB, GRP_DEV), F32),
            D((10,)),
            D((NCHUNK,)),
            D((3,)),
            D((4, 3)),
            D((4, 3)),
            D((2, 2)),
            D((2,)),
            pltpu.SemaphoreType.REGULAR,
        ],
        compiler_params=pltpu.CompilerParams(
            collective_id=0, has_side_effects=True, vmem_limit_bytes=48 << 20
        ),
    )(
        source_cell,
        electric_start,
        magnetic_start,
        current_start,
        cotangent,
        level_set,
        material,
        basis.reshape(NB * KB, TILE),
        block_owner.reshape(1, NB),
        block_group.reshape(1, NB),
    )


def solution(mesh):
    return jax.shard_map(
        local,
        mesh=mesh,
        in_specs=(
            P(None, "by", "bx", "gz"),
            P(None, "by", "bx", "gz"),
            P(None, "by", "bx", "gz"),
            P(None, "by", "bx", "gz"),
            P("by", "bx", "gz"),
            P("by", "bx", "gz"),
            P(("bx", "by", "gz")),
            P(("bx", "by", "gz"), None, None),
            P(("bx", "by", "gz"), None),
            P(("bx", "by", "gz")),
        ),
        out_specs=(
            P(None, "by", "bx", "gz"),
            P(None, "by", "bx", "gz"),
            P(None, ("bx", "by", "gz")),
        ),
        check_vma=False,
    )
```

time: 178 us -> 57.4 us (0.32); the launches traced: 175 us -> 56.7 us
  starting transfers between devices: 86.5 us -> 0 us
  Pallas kernels: 0 us -> 46.2 us
  other arithmetic: 41.9 us -> 0 us
  local copies, waits for them, and re-layouts: 28.3 us -> 9.9 us
  matrix products: 10 us -> 0 us
  waiting for transfers between devices: 6.91 us -> 0 us
    ppermute x24 -> x0, starting transfers between devices: 64.8 us -> none  [passed_along(): return lax.ppermute(x, axis, pairs)]
    pallas_call x0 -> x1, Pallas kernels: none -> 46.2 us  [local(): pl.pallas_call(kernel, name='adjoint_step', out_shape=(jax.ShapeDtypeStru...]
    all_to_all x2 -> x0, starting transfers between devices: 21.7 us -> none  [the longest x1 11.3 us: local(): lax.all_to_all(send_ids, ('bx', 'by'), split_axis=1, concat_axis=1, tiled...]
    sub x27 -> x0, other arithmetic: 17.6 us -> none  [the longest x8 7.75 us: differ(): return neighbour - couple]
    slice x33 -> x0, local copies, waits for them, and re-layouts: 12.9 us -> none  [the longest x8 5.3 us: beside(): lax.slice_in_dim(couple, 1, length, axis=axis_dim)]
    dot_general x4 -> x0, matrix products: 10 us -> none  [the longest x1 6.71 us: local(): jnp.einsum('tfkc,tc->tfk', blocks, cell_tiles, preferred_element_type=jnp...]
    another operation x20 -> x0, local copies, waits for them, and re-layouts: 8.45 us -> none  [the longest x8 7.18 us: beside(): arrived = jnp.expand_dims(arrived, axis_dim)]
    unnamed x33 -> x21, local copies, waits for them, and re-layouts: 2.72 us -> 9.9 us
  transfers between devices with their start and end apart: 26 -> 0, of which waited for: 4 -> 0; matrix products, arithmetic and copies ran while one was open for 34% -> 0% of each run, Pallas kernels for 0% -> 0%
where the time goes in v1:
time: 57.4 us; the launch traced here: 56.7 us
  Pallas kernels  46.2 us (80%)
  local copies, waits for them, and re-layouts  9.9 us (17%)
  between operations  0.66 us (1%)
    pallas_call x1, Pallas kernels, local(): pl.pallas_call(kernel, name='adjoint_step', out_shape=(jax.ShapeDtypeStru...  46.2 us
    unnamed x21, local copies, waits for them, and re-layouts  9.9 us

profile of v1, /device:TPU:8, one launch (start us, length us, event | category | flops | bytes accessed | tf_op | source)
XLA Modules:
  0.0 56.7 jit_solution(1349568857612326596)
XLA Ops:
  0.6 0.0 copy-start
  0.6 1.0 %copy-done = f32[3,16,16,128]{3,2,1,0:T(8,128)S(1)} copy-done((f32[3,16,16,128]{3,2,1,0:T(8,128)S(1)}, f32[3,16,16,128]{3,2,1,0:T(8,128)}, u32[]{:S(2)}) %copy-start) | copy-done | bytes 393240
  1.6 0.0 copy-start.1
  1.6 1.0 %copy-done.1 = f32[3,16,16,128]{3,2,1,0:T(8,128)S(1)} copy-done((f32[3,16,16,128]{3,2,1,0:T(8,128)S(1)}, f32[3,16,16,128]{3,2,1,0:T(8,128)}, u32[]{:S(2)}) %copy-start.1) | copy-done | bytes 393240
  2.6 0.0 copy-start.2
  2.6 1.0 %copy-done.2 = f32[3,16,16,128]{3,2,1,0:T(8,128)S(1)} copy-done((f32[3,16,16,128]{3,2,1,0:T(8,128)S(1)}, f32[3,16,16,128]{3,2,1,0:T(8,128)}, u32[]{:S(2)}) %copy-start.2) | copy-done | bytes 393240
  3.6 0.0 copy-start.3
  3.6 1.0 %copy-done.3 = f32[3,16,16,128]{3,2,1,0:T(8,128)S(1)} copy-done((f32[3,16,16,128]{3,2,1,0:T(8,128)S(1)}, f32[3,16,16,128]{3,2,1,0:T(8,128)}, u32[]{:S(2)}) %copy-start.3) | copy-done | bytes 393240
  4.6 0.0 copy-start.4
  4.6 0.9 %copy-done.4 = f32[16,16,128]{2,1,0:T(8,128)S(1)} copy-done((f32[16,16,128]{2,1,0:T(8,128)S(1)}, f32[16,16,128]{2,1,0:T(8,128)}, u32[]{:S(2)}) %copy-start.4) | copy-done | bytes 131096
  5.5 0.0 copy-start.5
  5.5 0.9 %copy-done.5 = s32[16,16,128]{2,1,0:T(8,128)S(1)} copy-done((s32[16,16,128]{2,1,0:T(8,128)S(1)}, s32[16,16,128]{2,1,0:T(8,128)}, u32[]{:S(2)}) %copy-start.5) | copy-done | bytes 131096
  6.4 0.0 copy-start.6
  6.4 0.7 %copy-done.6 = s32[256,1]{0,1:T(1,128)S(1)} copy-done((s32[256,1]{0,1:T(1,128)S(1)}, s32[256,1]{0,1:T(1,128)}, u32[]{:S(2)}) %copy-start.6) | copy-done | bytes 1048
  7.1 0.0 copy-start.7
  7.1 0.7 %copy-done.7 = s32[256]{0:T(256)S(1)} copy-done((s32[256]{0:T(256)S(1)}, s32[256]{0:T(256)}, u32[]{:S(2)}) %copy-start.7) | copy-done | bytes 1048
  7.8 0.0 copy-start.8
  7.8 0.7 %copy-done.8 = s32[8]{0:T(128)S(1)} copy-done((s32[8]{0:T(128)S(1)}, s32[8]{0:T(128)}, u32[]{:S(2)}) %copy-start.8) | copy-done | bytes 56
  8.4 46.2 %adjoint_step.1 = (f32[3,16,16,128]{3,2,1,0:T(8,128)S(1)}, f32[3,16,16,128]{3,2,1,0:T(8,128)S(1)}, f32[64,128]{1,0:T(8,128)S(1)}) custom-call(s32[8]{0:T(128)S(1)} %copy-done.8, f32[3,16,16,128]{3,2,1,0:T(8,128)S(1)} %copy-done, f32[3,16,16,128]{3,2,1,0:T(8,128)S(1)} %copy-done.1, f32[3,16,16,128]{3,2,1,0:T(8,128)S(1)} %copy-done.2, ...), custom_call_target="tpu_custom_call" | custom-call | tf_op jit(solution)/shard_map/adjoint_step/pallas_call | solution.py:514
  54.6 0.7 %copy.16 = f32[3,16,16,128]{3,2,1,0:T(8,128)} copy(f32[3,16,16,128]{3,2,1,0:T(8,128)S(1)} %get-tuple-element.6) | data formatting | bytes 786432
  55.4 0.7 %copy.17 = f32[3,16,16,128]{3,2,1,0:T(8,128)} copy(f32[3,16,16,128]{3,2,1,0:T(8,128)S(1)} %get-tuple-element.7) | data formatting | bytes 786432
  56.1 0.6 %copy.18 = f32[64,128]{1,0:T(8,128)} copy(f32[64,128]{1,0:T(8,128)S(1)} %get-tuple-element.8) | data formatting | bytes 65536
Async XLA Ops:
  0.6 1.0 %copy-start = (f32[3,16,16,128]{3,2,1,0:T(8,128)S(1)}, f32[3,16,16,128]{3,2,1,0:T(8,128)}, u32[]{:S(2)}) copy-start(f32[3,16,16,128]{3,2,1,0:T(8,128)} %e0_hbm.1) | copy-start | bytes 1179652
  1.6 1.0 %copy-start.1 = (f32[3,16,16,128]{3,2,1,0:T(8,128)S(1)}, f32[3,16,16,128]{3,2,1,0:T(8,128)}, u32[]{:S(2)}) copy-start(f32[3,16,16,128]{3,2,1,0:T(8,128)} %h0_hbm.1) | copy-start | bytes 1179652
  2.6 1.0 %copy-start.2 = (f32[3,16,16,128]{3,2,1,0:T(8,128)S(1)}, f32[3,16,16,128]{3,2,1,0:T(8,128)}, u32[]{:S(2)}) copy-start(f32[3,16,16,128]{3,2,1,0:T(8,128)} %j0_hbm.1) | copy-start | bytes 1179652
  3.6 1.0 %copy-start.3 = (f32[3,16,16,128]{3,2,1,0:T(8,128)S(1)}, f32[3,16,16,128]{3,2,1,0:T(8,128)}, u32[]{:S(2)}) copy-start(f32[3,16,16,128]{3,2,1,0:T(8,128)} %cot_hbm.1) | copy-start | bytes 1179652
  4.6 0.9 %copy-start.4 = (f32[16,16,128]{2,1,0:T(8,128)S(1)}, f32[16,16,128]{2,1,0:T(8,128)}, u32[]{:S(2)}) copy-start(f32[16,16,128]{2,1,0:T(8,128)} %level_hbm.1) | copy-start | bytes 393220
  5.5 0.9 %copy-start.5 = (s32[16,16,128]{2,1,0:T(8,128)S(1)}, s32[16,16,128]{2,1,0:T(8,128)}, u32[]{:S(2)}) copy-start(s32[16,16,128]{2,1,0:T(8,128)} %material_hbm.1) | copy-start | bytes 393220
  6.4 0.7 %copy-start.6 = (s32[256,1]{0,1:T(1,128)S(1)}, s32[256,1]{0,1:T(1,128)}, u32[]{:S(2)}) copy-start(s32[256,1]{0,1:T(1,128)} %param.18) | copy-start | bytes 3076
  7.1 0.7 %copy-start.7 = (s32[256]{0:T(256)S(1)}, s32[256]{0:T(256)}, u32[]{:S(2)}) copy-start(s32[256]{0:T(256)} %param.19) | copy-start | bytes 3076
  7.8 0.7 %copy-start.8 = (s32[8]{0:T(128)S(1)}, s32[8]{0:T(128)}, u32[]{:S(2)}) copy-start(s32[8]{0:T(128)} %source_ref.1) | copy-start | bytes 100

commit v2 on v1

--- a/solution.py
+++ b/solution.py
@@ -68,7 +68,6 @@
     silver,
     factor,
     sources,
-    d1,
     adj1,
     part1,
     grad,
@@ -509,7 +508,7 @@
 ):
     field = (3, 16, 16, 128)
     brick = (16, 16, 128)
-    anywhere = pl.BlockSpec(memory_space=pl.ANY)
+    anywhere = pl.BlockSpec(memory_space=pltpu.HBM)
     V, D = pltpu.VMEM, pltpu.SemaphoreType.DMA
     return pl.pallas_call(
         kernel,
@@ -535,7 +534,6 @@
             V(brick, F32),
             V(brick, F32),
             V(brick, F32),
-            V((8, 128), F32),
             V(field, F32),
             V(brick, F32),
             V((256, 128), F32),
@@ -565,7 +563,7 @@
             pltpu.SemaphoreType.REGULAR,
         ],
         compiler_params=pltpu.CompilerParams(
-            collective_id=0, has_side_effects=True, vmem_limit_bytes=48 << 20
+            collective_id=0, has_side_effects=True, vmem_limit_bytes=56000 << 10
         ),
     )(
         source_cell,

time: 57.4 us -> 51.3 us (0.89)
  local copies, waits for them, and re-layouts: 9.9 us -> 4.91 us
  Pallas kernels: 46.2 us -> 45.3 us
    unnamed x21 -> x3, local copies, waits for them, and re-layouts: 9.9 us -> 4.91 us
    pallas_call x1, Pallas kernels: 46.2 us -> 45.3 us  [local(): pl.pallas_call(kernel, name='adjoint_step', out_shape=(jax.ShapeDtypeStru...]
where the time goes in v2:
time: 51.3 us; the launch traced here: 50.9 us
  Pallas kernels  45.3 us (88%)
  local copies, waits for them, and re-layouts  4.91 us (10%)
  between operations  0.64 us (1%)
    pallas_call x1, Pallas kernels, local(): pl.pallas_call(kernel, name='adjoint_step', out_shape=(jax.ShapeDtypeStru...  45.3 us
    unnamed x3, local copies, waits for them, and re-layouts  4.91 us

profile of v2, /device:TPU:8, one launch (start us, length us, event | category | flops | bytes accessed | tf_op | source)
XLA Modules:
  0.0 50.9 jit_solution(16690643153170465575)
XLA Ops:
  0.6 45.3 %adjoint_step.1 = (f32[3,16,16,128]{3,2,1,0:T(8,128)}, f32[3,16,16,128]{3,2,1,0:T(8,128)}, f32[64,128]{1,0:T(8,128)}) custom-call(s32[8]{0:T(128)} %source_ref.1, f32[3,16,16,128]{3,2,1,0:T(8,128)} %e0_hbm.1, f32[3,16,16,128]{3,2,1,0:T(8,128)} %h0_hbm.1, f32[3,16,16,128]{3,2,1,0:T(8,128)} %j0_hbm.1, f32[3,16,16,128]{3,2,1,0:T(8,128)} %cot_hbm.1, ...), custom_call_target="tpu_custom_call" | custom-call | tf_op jit(solution)/shard_map/adjoint_step/pallas_call | solution.py:513
  46.0 1.8 %copy.16 = f32[3,16,16,128]{3,2,1,0:T(8,128)} copy(f32[3,16,16,128]{3,2,1,0:T(8,128)} %get-tuple-element.6) | data formatting | bytes 786432
  47.7 1.8 %copy.17 = f32[3,16,16,128]{3,2,1,0:T(8,128)} copy(f32[3,16,16,128]{3,2,1,0:T(8,128)} %get-tuple-element.7) | data formatting | bytes 786432
  49.5 1.4 %copy.18 = f32[64,128]{1,0:T(8,128)} copy(f32[64,128]{1,0:T(8,128)} %get-tuple-element.8) | data formatting | bytes 65536

commit v3 on v2

--- a/solution.py
+++ b/solution.py
@@ -84,8 +84,6 @@
     partial,
     vsend,
     vrecv,
-    isend,
-    irecv,
     coef,
     in_sem,
     basis_sem,
@@ -228,9 +226,12 @@
         for out, _, c in moves(r, field):
             pl.when(out)(c.start)
 
-    def receive(r, field):
-        for out, into, c in moves(r, field):
+    def receive(r, field, first, last):
+        for _, into, c in moves(r, field)[first:last]:
             pl.when(into)(c.wait_recv)
+
+    def sent(r, field):
+        for out, _, c in moves(r, field):
             pl.when(out)(c.wait_send)
 
     send(0, p1)
@@ -265,7 +266,7 @@
         pick = block == 2 * tile + f
         targets.append(jnp.sum(jnp.where(pick, target_col, 0.0), axis=0, keepdims=True))
         groups.append(jnp.sum(jnp.where(pick, group_col, 0.0), axis=0, keepdims=True))
-    slot_row = (2 * iota((NB, TILES), 0)).astype(F32)
+    slot_row = (4 * (block % PLANES) + 2 * (block // PLANES)).astype(F32)
     for h in range(2):
         for f in range(2):
             place[:, pl.ds((2 * h + f) * TILES, TILES)] = (
@@ -277,7 +278,7 @@
         for f in range(2):
             hit = hit + jnp.where(targets[f] == first_slot + float(s), groups[f], 0.0)
         id_sum = jnp.where(id_lane == s, jnp.sum(hit, axis=1, keepdims=True), id_sum)
-    isend[:, 0, :] = id_sum
+    vsend[pl.ds(2, PLANES, stride=3), 0, :] = id_sum
 
     def plus_half(r, field, old, out):
         nxt = r + 1
@@ -307,7 +308,10 @@
                 xsend[nxt, i, pl.ds(y, 1), :] = vals[k][15:16]
             return pack_z(acc, y, [vals[k] for k in (("x", 0), ("y", 0), ("x", 1), ("y", 1))], 127)
 
-        zsend[nxt] = lax.fori_loop(0, 16, body, jnp.zeros((16, 128), F32))
+        receive(r, field, 1, 3)
+        acc = lax.fori_loop(0, 15, body, jnp.zeros((16, 128), F32))
+        receive(r, field, 0, 1)
+        zsend[nxt] = body(15, acc)
 
     def minus_turn(r, field, y, s):
         zf = zrecv[r]
@@ -332,42 +336,39 @@
         before = m1[IDX[(c, s)], y + 1]
         return before + turn if s else before - time_step * turn
 
-    receive(0, p1)
     plus_half(0, p1, old_first, m1)
     send(1, m1)
 
-    pl.semaphore_wait(ready_sem, 15)
-
-    def spread(src, dst, width, k):
+    def chunk(p):
+        return pl.ds(p * 3, 3)
+
+    def mine():
+        return pltpu.make_async_copy(vsend.at[chunk(me)], vrecv.at[chunk(me)], own_sem)
+
+    def spread():
         def one(i, _):
             p = (me + i) % PLANES
             pltpu.make_async_remote_copy(
-                src_ref=src.at[pl.ds(p * width, width)],
-                dst_ref=dst.at[pl.ds(me * width, width)],
-                send_sem=a2a_sem.at[k, 0],
-                recv_sem=a2a_sem.at[k, 1],
+                src_ref=vsend.at[chunk(p)],
+                dst_ref=vrecv.at[chunk(me)],
+                send_sem=a2a_sem.at[0],
+                recv_sem=a2a_sem.at[1],
                 device_id={"bx": p // NBY, "by": p % NBY},
                 device_id_type=MESH,
             ).start()
             return 0
 
-        own = pltpu.make_async_copy(
-            src.at[pl.ds(me * width, width)], dst.at[pl.ds(me * width, width)], own_sem.at[k]
-        )
-        own.start()
+        mine().start()
         lax.fori_loop(1, PLANES, one, 0, unroll=4)
 
-    def gathered(src, dst, width, k):
-        many = pl.ds(0, (PLANES - 1) * width)
-        pltpu.make_async_copy(src.at[many], src.at[many], a2a_sem.at[k, 0]).wait()
-        pltpu.make_async_copy(dst.at[many], dst.at[many], a2a_sem.at[k, 1]).wait()
-        pltpu.make_async_copy(
-            src.at[pl.ds(me * width, width)], dst.at[pl.ds(me * width, width)], own_sem.at[k]
-        ).wait()
-
-    spread(isend, irecv, 1, 0)
-
-    receive(1, m1)
+    def gathered():
+        many = pl.ds(0, (PLANES - 1) * 3)
+        pltpu.make_async_copy(vrecv.at[many], vrecv.at[many], a2a_sem.at[1]).wait()
+        mine().wait()
+
+    def all_sent():
+        many = pl.ds(0, (PLANES - 1) * 3)
+        pltpu.make_async_copy(vsend.at[many], vsend.at[many], a2a_sem.at[0]).wait()
 
     def electric_first(y, acc):
         rat, sil = ratio[y], silver[y]
@@ -396,12 +397,13 @@
             xsend[2, i, pl.ds(y, 1), :] = v[0:1]
         return pack_z(acc, y, (fwd["x"], fwd["y"], adj["x"], adj["y"]), 0)
 
-    zsend[2] = lax.fori_loop(0, 16, electric_first, jnp.zeros((16, 128), F32))
+    receive(1, m1, 1, 3)
+    pack = lax.fori_loop(1, 16, electric_first, jnp.zeros((16, 128), F32))
+    receive(1, m1, 0, 1)
+    zsend[2] = electric_first(0, pack)
     send(2, p2)
-    receive(2, p2)
     plus_half(2, p2, old_second, m2)
     send(3, m2)
-    receive(3, m2)
 
     def electric_second(y, _):
         rat, sil = ratio[y], silver[y]
@@ -423,7 +425,10 @@
         grad[pl.ds(pl.multiple_of(y * 16, 16), 16), :] = factor[y] * total
         return 0
 
-    lax.fori_loop(0, 16, electric_second, 0)
+    receive(3, m2, 1, 3)
+    lax.fori_loop(1, 16, electric_second, 0)
+    receive(3, m2, 0, 1)
+    electric_second(0, 0)
     outs = [
         pltpu.make_async_copy(efin, e_out, out_sem.at[0]),
         pltpu.make_async_copy(afin, a_out, out_sem.at[1]),
@@ -466,11 +471,13 @@
     hi, lo = split(stack)
     slots = lax.dot_general(place[...], hi, (((1,), (0,)), ((), ())), preferred_element_type=F32)
     slots = slots + lax.dot_general(place[...], lo, (((1,), (0,)), ((), ())), preferred_element_type=F32)
-    vsend[:, 0, :] = slots
-    spread(vsend, vrecv, 2, 1)
-
-    gathered(isend, irecv, 1, 0)
-    ids = irecv[:, 0, :]
+    for p in range(2):
+        vsend[pl.ds(p, PLANES, stride=3), 0, :] = slots[p * PLANES : (p + 1) * PLANES]
+    pl.semaphore_wait(ready_sem, 15)
+    spread()
+
+    gathered()
+    ids = vrecv[pl.ds(2, PLANES, stride=3), 0, :]
     group_lane = iota((PLANES, GRP_DEV), 1).astype(F32)
     hits = jnp.concatenate(
         [
@@ -481,8 +488,7 @@
         ],
         axis=0,
     )
-    gathered(vsend, vrecv, 2, 1)
-    vals = jnp.concatenate([vrecv[pl.ds(p, PLANES, stride=2), 0, :] for p in range(2)], axis=0)
+    vals = jnp.concatenate([vrecv[pl.ds(p, PLANES, stride=3), 0, :] for p in range(2)], axis=0)
     hi, lo = split(vals)
     both = lax.dot_general(hi, hits, (((0,), (0,)), ((), ())), preferred_element_type=F32)
     both = both + lax.dot_general(lo, hits, (((0,), (0,)), ((), ())), preferred_element_type=F32)
@@ -491,6 +497,9 @@
     last.start()
     for c in outs:
         c.wait()
+    for r, field in enumerate((p1, m1, p2, m2)):
+        sent(r, field)
+    all_sent()
     last.wait()
 
 
@@ -548,18 +557,16 @@
             V((4, 16, 128), F32),
             V((NB, 4 * TILES), BF16),
             V((TILES, 128), F32),
-            V((NB, 1, 128), F32),
-            V((NB, 1, 128), F32),
-            V((PLANES, 1, 128), F32),
-            V((PLANES, 1, 128), F32),
+            V((3 * PLANES, 1, 128), F32),
+            V((3 * PLANES, 1, 128), F32),
             V((KB, GRP_DEV), F32),
             D((10,)),
             D((NCHUNK,)),
             D((3,)),
             D((4, 3)),
             D((4, 3)),
-            D((2, 2)),
             D((2,)),
+            D,
             pltpu.SemaphoreType.REGULAR,
         ],
         compiler_params=pltpu.CompilerParams(

time: 51.3 us -> 49.3 us (0.961)
  Pallas kernels: 45.3 us -> 43.4 us
    pallas_call x1, Pallas kernels: 45.3 us -> 43.4 us  [local(): pl.pallas_call(kernel, name='adjoint_step', out_shape=(jax.ShapeDtypeStru...]
where the time goes in v3:
time: 49.3 us; the launch traced here: 49 us
  Pallas kernels  43.4 us (88%)
  local copies, waits for them, and re-layouts  4.91 us (10%)
  between operations  0.64 us (1%)
    pallas_call x1, Pallas kernels, local(): pl.pallas_call(kernel, name='adjoint_step', out_shape=(jax.ShapeDtypeStru...  43.4 us
    unnamed x3, local copies, waits for them, and re-layouts  4.91 us

profile of v3, /device:TPU:8, one launch (start us, length us, event | category | flops | bytes accessed | tf_op | source)
XLA Modules:
  0.0 49.0 jit_solution(1519223599959763844)
XLA Ops:
  0.6 43.4 %adjoint_step.1 = (f32[3,16,16,128]{3,2,1,0:T(8,128)}, f32[3,16,16,128]{3,2,1,0:T(8,128)}, f32[64,128]{1,0:T(8,128)}) custom-call(s32[8]{0:T(128)} %source_ref.1, f32[3,16,16,128]{3,2,1,0:T(8,128)} %e0_hbm.1, f32[3,16,16,128]{3,2,1,0:T(8,128)} %h0_hbm.1, f32[3,16,16,128]{3,2,1,0:T(8,128)} %j0_hbm.1, f32[3,16,16,128]{3,2,1,0:T(8,128)} %cot_hbm.1, ...), custom_call_target="tpu_custom_call" | custom-call | tf_op jit(solution)/shard_map/adjoint_step/pallas_call | solution.py:522
  44.1 1.8 %copy.16 = f32[3,16,16,128]{3,2,1,0:T(8,128)} copy(f32[3,16,16,128]{3,2,1,0:T(8,128)} %get-tuple-element.6) | data formatting | bytes 786432
  45.8 1.8 %copy.17 = f32[3,16,16,128]{3,2,1,0:T(8,128)} copy(f32[3,16,16,128]{3,2,1,0:T(8,128)} %get-tuple-element.7) | data formatting | bytes 786432
  47.6 1.4 %copy.18 = f32[64,128]{1,0:T(8,128)} copy(f32[64,128]{1,0:T(8,128)} %get-tuple-element.8) | data formatting | bytes 65536

commit v4 on v3

--- a/solution.py
+++ b/solution.py
@@ -186,7 +186,7 @@
             xsend[0, c, pl.ds(y, 1), :] = v[0:1]
         return pack_z(acc, y, (ex, ey, sx, sy), 0)
 
-    zsend[0] = lax.fori_loop(0, 16, first, jnp.zeros((16, 128), F32))
+    zsend[0] = lax.fori_loop(0, 16, first, jnp.zeros((16, 128), F32), unroll=4)
 
     pl.semaphore_wait(barrier, 23 + up_far.astype(jnp.int32) + down_far.astype(jnp.int32))
     for i in range(1, 16):
@@ -247,7 +247,7 @@
         sources[y] = total
         return 0
 
-    lax.fori_loop(0, 16, count, 0)
+    lax.fori_loop(0, 16, count, 0, unroll=4)
 
     owner_row = owner[...].astype(F32)
     group_row = group[...].astype(F32)
@@ -309,7 +309,7 @@
             return pack_z(acc, y, [vals[k] for k in (("x", 0), ("y", 0), ("x", 1), ("y", 1))], 127)
 
         receive(r, field, 1, 3)
-        acc = lax.fori_loop(0, 15, body, jnp.zeros((16, 128), F32))
+        acc = lax.fori_loop(0, 15, body, jnp.zeros((16, 128), F32), unroll=5)
         receive(r, field, 0, 1)
         zsend[nxt] = body(15, acc)
 
@@ -398,7 +398,7 @@
         return pack_z(acc, y, (fwd["x"], fwd["y"], adj["x"], adj["y"]), 0)
 
     receive(1, m1, 1, 3)
-    pack = lax.fori_loop(1, 16, electric_first, jnp.zeros((16, 128), F32))
+    pack = lax.fori_loop(1, 16, electric_first, jnp.zeros((16, 128), F32), unroll=5)
     receive(1, m1, 0, 1)
     zsend[2] = electric_first(0, pack)
     send(2, p2)
@@ -426,7 +426,7 @@
         return 0
 
     receive(3, m2, 1, 3)
-    lax.fori_loop(1, 16, electric_second, 0)
+    lax.fori_loop(1, 16, electric_second, 0, unroll=5)
     receive(3, m2, 0, 1)
     electric_second(0, 0)
     outs = [
@@ -454,7 +454,7 @@
         partial[pl.ds(start, 16), :] = jnp.where(row % 2 == 0, acc[:, :128], acc[:, 128:])
         return 0
 
-    lax.fori_loop(0, 8, tiles, 0)
+    lax.fori_loop(0, 8, tiles, 0, unroll=2)
 
     part = partial[...]
     turned = pltpu.roll(part, 64, 1)

time: 49.3 us -> 43.7 us (0.89)
  Pallas kernels: 43.4 us -> 37.9 us
    pallas_call x1, Pallas kernels: 43.4 us -> 37.9 us  [local(): pl.pallas_call(kernel, name='adjoint_step', out_shape=(jax.ShapeDtypeStru...]
where the time goes in v4:
time: 43.7 us; the launch traced here: 43.4 us
  Pallas kernels  37.9 us (87%)
  local copies, waits for them, and re-layouts  4.91 us (11%)
  between operations  0.64 us (1%)
    pallas_call x1, Pallas kernels, local(): pl.pallas_call(kernel, name='adjoint_step', out_shape=(jax.ShapeDtypeStru...  37.9 us
    unnamed x3, local copies, waits for them, and re-layouts  4.91 us

profile of v4, /device:TPU:8, one launch (start us, length us, event | category | flops | bytes accessed | tf_op | source)
XLA Modules:
  0.0 43.4 jit_solution(12836597619075950226)
XLA Ops:
  0.6 37.9 %adjoint_step.1 = (f32[3,16,16,128]{3,2,1,0:T(8,128)}, f32[3,16,16,128]{3,2,1,0:T(8,128)}, f32[64,128]{1,0:T(8,128)}) custom-call(s32[8]{0:T(128)} %source_ref.1, f32[3,16,16,128]{3,2,1,0:T(8,128)} %e0_hbm.1, f32[3,16,16,128]{3,2,1,0:T(8,128)} %h0_hbm.1, f32[3,16,16,128]{3,2,1,0:T(8,128)} %j0_hbm.1, f32[3,16,16,128]{3,2,1,0:T(8,128)} %cot_hbm.1, ...), custom_call_target="tpu_custom_call" | custom-call | tf_op jit(solution)/shard_map/adjoint_step/pallas_call | solution.py:522
  38.5 1.8 %copy.16 = f32[3,16,16,128]{3,2,1,0:T(8,128)} copy(f32[3,16,16,128]{3,2,1,0:T(8,128)} %get-tuple-element.6) | data formatting | bytes 786432
  40.3 1.8 %copy.17 = f32[3,16,16,128]{3,2,1,0:T(8,128)} copy(f32[3,16,16,128]{3,2,1,0:T(8,128)} %get-tuple-element.7) | data formatting | bytes 786432
  42.1 1.4 %copy.18 = f32[64,128]{1,0:T(8,128)} copy(f32[64,128]{1,0:T(8,128)} %get-tuple-element.8) | data formatting | bytes 65536

commit v5 on v4

--- a/solution.py
+++ b/solution.py
@@ -27,7 +27,7 @@
 BF16 = jnp.bfloat16
 MESH = pl.DeviceIdType.MESH
 
-IDX = {("x", 0): 0, ("z", 0): 1, ("x", 1): 2, ("z", 1): 3, ("y", 0): 4, ("y", 1): 5}
+IDX = {("x", 0): 0, ("z", 0): 1, ("y", 0): 2, ("x", 1): 3, ("z", 1): 4, ("y", 1): 5}
 COMP = {"x": 0, "y": 1, "z": 2}
 
 
@@ -69,6 +69,7 @@
     factor,
     sources,
     adj1,
+    drive1,
     part1,
     grad,
     efin,
@@ -97,7 +98,6 @@
     bx, by, gz = lax.axis_index("bx"), lax.axis_index("by"), lax.axis_index("gz")
     me = bx * NBY + by
     yy, zz = by // 8, by % 8
-    xy = bx * 4 + yy
 
     loads = [
         (material_hbm, material),
@@ -105,7 +105,7 @@
         (cot_hbm, cot),
         (e0_hbm.at[0], p1.at[0, pl.ds(0, 16)]),
         (e0_hbm.at[2], p1.at[1, pl.ds(0, 16)]),
-        (e0_hbm.at[1], p1.at[4, pl.ds(0, 16)]),
+        (e0_hbm.at[1], p1.at[2, pl.ds(0, 16)]),
         (h0_hbm, h0),
         (j0_hbm, j0),
         (owner_hbm, owner),
@@ -115,12 +115,14 @@
     for c in loads:
         c.start()
 
-    zrow = jnp.zeros((4, 16, 128), F32)
+    zrow = jnp.zeros((2, 16, 128), F32)
     for ref, at in ((p1, 16), (p2, 16), (m1, 0), (m2, 0)):
-        ref[0:4, at] = zrow
+        for t in range(2):
+            ref[3 * t : 3 * t + 2, at] = zrow
     for r in range(4):
-        xrecv[r] = zrow
-        zrecv[r] = jnp.zeros((16, 128), F32)
+        for t in range(2):
+            xrecv[r, t] = zrow
+        zrecv[r] = zrow
 
     barrier = pltpu.get_barrier_semaphore()
 
@@ -129,9 +131,9 @@
 
     for i in range(1, 8):
         hail(by=yy * 8 + (zz + i) % 8)
-    for i in range(1, 16):
-        q = (xy + i) % 16
-        hail(bx=q // 4, by=(q % 4) * 8 + zz)
+    for i in range(1, 4):
+        hail(by=(yy + i) % 4 * 8 + zz)
+        hail(bx=(bx + i) % 4)
     hail(gz=1 - gz)
     up_far = jnp.logical_and(zz == 7, by < NBY - 1)
     down_far = jnp.logical_and(zz == 0, by > 0)
@@ -162,7 +164,7 @@
 
     def pack_z(acc, y, vals, from_lane):
         for c, v in enumerate(vals):
-            at = 4 * y + c
+            at = 2 * y + c
             acc = jnp.where(lane == at, pltpu.roll(v, (at + 128 - from_lane) % 128, 1), acc)
         return acc
 
@@ -170,32 +172,33 @@
         mat = material[y]
         lev = level[y]
         smooth = jax.nn.sigmoid(lev)
-        design = (mat == 1).astype(F32)
         sil = (mat == 2).astype(F32)
         permit = jnp.where(mat == 2, metal_permit, jnp.where(mat == 1, 1.0 + design_contrast * smooth, 1.0))
         rat = time_step / permit
         ratio[y] = rat
         silver[y] = sil
-        factor[y] = -(design * design_contrast * (smooth * (1.0 - smooth))) / permit
         sx, sy, sz = (rat * cot[c, y] for c in range(3))
-        p1[2, y] = sx
-        p1[3, y] = sz
+        p1[3, y] = sx
+        p1[4, y] = sz
         p1[5, y] = sy
-        ex, ey, ez = p1[0, y], p1[4, y], p1[1, y]
-        for c, v in enumerate((ey, ez, sy, sz)):
-            xsend[0, c, pl.ds(y, 1), :] = v[0:1]
-        return pack_z(acc, y, (ex, ey, sx, sy), 0)
-
-    zsend[0] = lax.fori_loop(0, 16, first, jnp.zeros((16, 128), F32), unroll=4)
-
-    pl.semaphore_wait(barrier, 23 + up_far.astype(jnp.int32) + down_far.astype(jnp.int32))
-    for i in range(1, 16):
-        q = (xy + i) % 16
+        ex, ey, ez = p1[0, y], p1[2, y], p1[1, y]
+        for t, couple in enumerate(((ey, ez), (sy, sz))):
+            for c, v in enumerate(couple):
+                xsend[0, t, c, pl.ds(y, 1), :] = v[0:1]
+        return pack_z(acc[0], y, (ex, ey), 0), pack_z(acc[1], y, (sx, sy), 0)
+
+    empty = jnp.zeros((16, 128), F32)
+    packs = lax.fori_loop(0, 16, first, (empty, empty), unroll=4)
+    for t in range(2):
+        zsend[0, t] = packs[t]
+
+    pl.semaphore_wait(barrier, 14 + up_far.astype(jnp.int32) + down_far.astype(jnp.int32))
+    for i in range(1, 4):
         pl.semaphore_signal(
-            ready_sem, inc=1, device_id={"bx": q // 4, "by": (q % 4) * 8 + zz}, device_id_type=MESH
+            ready_sem.at[0], inc=1, device_id={"by": (yy + i) % 4 * 8 + zz}, device_id_type=MESH
         )
 
-    def moves(r, field):
+    def moves(r, t, field):
         plus = r % 2 == 0
         step = -1 if plus else 1
         edge, halo = (0, 16) if plus else (16, 0)
@@ -204,8 +207,8 @@
             return pltpu.make_async_remote_copy(
                 src_ref=src,
                 dst_ref=dst,
-                send_sem=send_sem.at[r, i],
-                recv_sem=recv_sem.at[r, i],
+                send_sem=send_sem.at[2 * r + t, i],
+                recv_sem=recv_sem.at[2 * r + t, i],
                 device_id=where,
                 device_id_type=MESH,
             )
@@ -217,24 +220,25 @@
         z_out = gz == 1 if plus else gz == 0
         z_in = gz == 0 if plus else gz == 1
         return (
-            (y_out, y_in, move(field.at[pl.ds(0, 4), edge], field.at[pl.ds(0, 4), halo], 0, by=by + step)),
-            (x_out, x_in, move(xsend.at[r], xrecv.at[r], 1, bx=bx + step)),
-            (z_out, z_in, move(zsend.at[r], zrecv.at[r], 2, gz=1 - gz)),
+            (y_out, y_in, move(field.at[pl.ds(3 * t, 2), edge], field.at[pl.ds(3 * t, 2), halo], 0, by=by + step)),
+            (x_out, x_in, move(xsend.at[r, t], xrecv.at[r, t], 1, bx=bx + step)),
+            (z_out, z_in, move(zsend.at[r, t], zrecv.at[r, t], 2, gz=1 - gz)),
         )
 
-    def send(r, field):
-        for out, _, c in moves(r, field):
+    def send(r, t, field):
+        for out, _, c in moves(r, t, field):
             pl.when(out)(c.start)
 
-    def receive(r, field, first, last):
-        for _, into, c in moves(r, field)[first:last]:
+    def receive(r, t, field, first, last):
+        for _, into, c in moves(r, t, field)[first:last]:
             pl.when(into)(c.wait_recv)
 
-    def sent(r, field):
-        for out, _, c in moves(r, field):
+    def sent(r, t, field):
+        for out, _, c in moves(r, t, field):
             pl.when(out)(c.wait_send)
 
-    send(0, p1)
+    send(0, 0, p1)
+    send(0, 1, p1)
 
     for c in loads[6:]:
         c.wait()
@@ -245,6 +249,9 @@
         for i in range(8):
             total = total + (flat == source_ref[i]).astype(F32)
         sources[y] = total
+        smooth = jax.nn.sigmoid(level[y])
+        design = (material[y] == 1).astype(F32)
+        factor[y] = -(design * design_contrast * (smooth * (1.0 - smooth))) * (ratio[y] * (1.0 / time_step))
         return 0
 
     lax.fori_loop(0, 16, count, 0, unroll=4)
@@ -280,53 +287,51 @@
         id_sum = jnp.where(id_lane == s, jnp.sum(hit, axis=1, keepdims=True), id_sum)
     vsend[pl.ds(2, PLANES, stride=3), 0, :] = id_sum
 
-    def plus_half(r, field, old, out):
+    def plus_half(r, t, field, old, out):
         nxt = r + 1
 
         def body(y, acc):
-            zf = zrecv[r]
+            zf = zrecv[r, t]
+            fx, fy, fz = (field[IDX[(c, t)], y] for c in "xyz")
+            dyx = field[IDX[("x", t)], y + 1] - fx
+            dyz = field[IDX[("z", t)], y + 1] - fz
+
+            def along_x(v, c):
+                return jnp.where(row == 15, xrecv[r, t, c, pl.ds(y, 1), :], pltpu.roll(v, 15, 0)) - v
+
+            def along_z(v, c):
+                return jnp.where(lane == 127, pltpu.roll(zf, 127 - 2 * y - c, 1), pltpu.roll(v, 127, 1)) - v
+
+            dxy, dxz = along_x(fy, 0), along_x(fz, 1)
+            dzx, dzy = along_z(fx, 0), along_z(fy, 1)
+            turn = {"x": dyz - dzy, "y": dzx - dxz, "z": dxy - dyx}
             vals = {}
-            for s in range(2):
-                fx, fy, fz = (field[IDX[(c, s)], y] for c in "xyz")
-                dyx = field[IDX[("x", s)], y + 1] - fx
-                dyz = field[IDX[("z", s)], y + 1] - fz
-
-                def along_x(v, c):
-                    return jnp.where(row == 15, xrecv[r, c, pl.ds(y, 1), :], pltpu.roll(v, 15, 0)) - v
-
-                def along_z(v, c):
-                    return jnp.where(lane == 127, pltpu.roll(zf, 127 - 4 * y - c, 1), pltpu.roll(v, 127, 1)) - v
-
-                dxy, dxz = along_x(fy, 2 * s), along_x(fz, 2 * s + 1)
-                dzx, dzy = along_z(fx, 2 * s), along_z(fy, 2 * s + 1)
-                turn = {"x": dyz - dzy, "y": dzx - dxz, "z": dxy - dyx}
-                for c in "xyz":
-                    new = old(s, c, y, turn[c])
-                    out[IDX[(c, s)], y + 1] = new
-                    vals[(c, s)] = new
-            for i, k in enumerate((("y", 0), ("z", 0), ("y", 1), ("z", 1))):
-                xsend[nxt, i, pl.ds(y, 1), :] = vals[k][15:16]
-            return pack_z(acc, y, [vals[k] for k in (("x", 0), ("y", 0), ("x", 1), ("y", 1))], 127)
-
-        receive(r, field, 1, 3)
-        acc = lax.fori_loop(0, 15, body, jnp.zeros((16, 128), F32), unroll=5)
-        receive(r, field, 0, 1)
-        zsend[nxt] = body(15, acc)
-
-    def minus_turn(r, field, y, s):
-        zf = zrecv[r]
-        fx, fy, fz = (field[IDX[(c, s)], y + 1] for c in "xyz")
-        dyx = fx - field[IDX[("x", s)], y]
-        dyz = fz - field[IDX[("z", s)], y]
+            for c in "xyz":
+                vals[c] = old(t, c, y, turn[c])
+                out[IDX[(c, t)], y + 1] = vals[c]
+            for i, c in enumerate("yz"):
+                xsend[nxt, t, i, pl.ds(y, 1), :] = vals[c][15:16]
+            return pack_z(acc, y, (vals["x"], vals["y"]), 127)
+
+        receive(r, t, field, 1, 3)
+        acc = lax.fori_loop(0, 15, body, empty, unroll=5)
+        receive(r, t, field, 0, 1)
+        zsend[nxt, t] = body(15, acc)
+
+    def minus_turn(r, t, field, y):
+        zf = zrecv[r, t]
+        fx, fy, fz = (field[IDX[(c, t)], y + 1] for c in "xyz")
+        dyx = fx - field[IDX[("x", t)], y]
+        dyz = fz - field[IDX[("z", t)], y]
 
         def along_x(v, c):
-            return v - jnp.where(row == 0, xrecv[r, c, pl.ds(y, 1), :], pltpu.roll(v, 1, 0))
+            return v - jnp.where(row == 0, xrecv[r, t, c, pl.ds(y, 1), :], pltpu.roll(v, 1, 0))
 
         def along_z(v, c):
-            return v - jnp.where(lane == 0, pltpu.roll(zf, 128 - 4 * y - c, 1), pltpu.roll(v, 1, 1))
-
-        dxy, dxz = along_x(fy, 2 * s), along_x(fz, 2 * s + 1)
-        dzx, dzy = along_z(fx, 2 * s), along_z(fy, 2 * s + 1)
+            return v - jnp.where(lane == 0, pltpu.roll(zf, 128 - 2 * y - c, 1), pltpu.roll(v, 1, 1))
+
+        dxy, dxz = along_x(fy, 0), along_x(fz, 1)
+        dzx, dzy = along_z(fx, 0), along_z(fy, 1)
         return {"x": dyz - dzy, "y": dzx - dxz, "z": dxy - dyx}
 
     def old_first(s, c, y, turn):
@@ -336,8 +341,13 @@
         before = m1[IDX[(c, s)], y + 1]
         return before + turn if s else before - time_step * turn
 
-    plus_half(0, p1, old_first, m1)
-    send(1, m1)
+    for t in range(2):
+        plus_half(0, t, p1, old_first, m1)
+        send(1, t, m1)
+
+    pl.semaphore_wait(ready_sem.at[0], 3)
+    for i in range(1, 4):
+        pl.semaphore_signal(ready_sem.at[1], inc=1, device_id={"bx": (bx + i) % 4}, device_id_type=MESH)
 
     def chunk(p):
         return pl.ds(p * 3, 3)
@@ -372,69 +382,65 @@
 
     def electric_first(y, acc):
         rat, sil = ratio[y], silver[y]
-        turn, back = minus_turn(1, m1, y, 0), minus_turn(1, m1, y, 1)
-        total = jnp.zeros((16, 128), F32)
-        fwd, adj = {}, {}
+        turn = minus_turn(1, 0, m1, y)
+        vals = {}
         for c in "xyz":
             e = p1[IDX[(c, 0)], y]
             cur = sil * (drude_keep * j0[COMP[c], y] + drude_gain * e)
             drive = turn[c] - cur
             j0[COMP[c], y] = cur
+            drive1[COMP[c], y] = drive
             new = e + rat * drive
             if c == "z":
                 new = new + source_level * source_wave[0] * sources[y]
-            fwd[c] = new
+            vals[c] = new
             p2[IDX[(c, 0)], y] = new
-            scaled = p1[IDX[(c, 1)], y]
-            a = cot[COMP[c], y] - drude_gain * (sil * scaled) - time_step * back[c]
+        for i, c in enumerate("yz"):
+            xsend[2, 0, i, pl.ds(y, 1), :] = vals[c][0:1]
+        return pack_z(acc, y, (vals["x"], vals["y"]), 0)
+
+    def adjoint_first(y, acc):
+        rat, sil = ratio[y], silver[y]
+        back = minus_turn(1, 1, m1, y)
+        total = jnp.zeros((16, 128), F32)
+        vals = {}
+        for c in "xyz":
+            a = cot[COMP[c], y] - drude_gain * (sil * p1[IDX[(c, 1)], y]) - time_step * back[c]
             adj1[COMP[c], y] = a
-            s0 = rat * a
-            adj[c] = s0
-            p2[IDX[(c, 1)], y] = s0
-            total = total + s0 * drive
+            vals[c] = rat * a
+            p2[IDX[(c, 1)], y] = vals[c]
+            total = total + vals[c] * drive1[COMP[c], y]
         part1[y] = total
-        for i, v in enumerate((fwd["y"], fwd["z"], adj["y"], adj["z"])):
-            xsend[2, i, pl.ds(y, 1), :] = v[0:1]
-        return pack_z(acc, y, (fwd["x"], fwd["y"], adj["x"], adj["y"]), 0)
-
-    receive(1, m1, 1, 3)
-    pack = lax.fori_loop(1, 16, electric_first, jnp.zeros((16, 128), F32), unroll=5)
-    receive(1, m1, 0, 1)
-    zsend[2] = electric_first(0, pack)
-    send(2, p2)
-    plus_half(2, p2, old_second, m2)
-    send(3, m2)
-
-    def electric_second(y, _):
-        rat, sil = ratio[y], silver[y]
-        turn, back = minus_turn(3, m2, y, 0), minus_turn(3, m2, y, 1)
+        for i, c in enumerate("yz"):
+            xsend[2, 1, i, pl.ds(y, 1), :] = vals[c][0:1]
+        return pack_z(acc, y, (vals["x"], vals["y"]), 0)
+
+    for t, body in enumerate((electric_first, adjoint_first)):
+        receive(1, t, m1, 1, 3)
+        pack = lax.fori_loop(1, 16, body, empty, unroll=5)
+        receive(1, t, m1, 0, 1)
+        zsend[2, t] = body(0, pack)
+        send(2, t, p2)
+    for t in range(2):
+        plus_half(2, t, p2, old_second, m2)
+        send(3, t, m2)
+
+    def drive_second(y, _):
+        sil = silver[y]
+        turn = minus_turn(3, 0, m2, y)
         total = part1[y]
         for c in "xyz":
-            e = p2[IDX[(c, 0)], y]
-            cur = sil * (drude_keep * j0[COMP[c], y] + drude_gain * e)
+            cur = sil * (drude_keep * j0[COMP[c], y] + drude_gain * p2[IDX[(c, 0)], y])
             drive = turn[c] - cur
-            new = e + rat * drive
-            if c == "z":
-                new = new + source_level * source_wave[1] * sources[y]
-            efin[COMP[c], y] = new
-            scaled = p1[IDX[(c, 1)], y]
-            s0 = p2[IDX[(c, 1)], y]
-            adj_drive = -drude_keep * (sil * scaled) - s0
-            afin[COMP[c], y] = adj1[COMP[c], y] + drude_gain * (sil * adj_drive) - time_step * back[c]
-            total = total + scaled * drive
+            efin[COMP[c], y] = drive
+            total = total + p1[IDX[(c, 1)], y] * drive
         grad[pl.ds(pl.multiple_of(y * 16, 16), 16), :] = factor[y] * total
         return 0
 
-    receive(3, m2, 1, 3)
-    lax.fori_loop(1, 16, electric_second, 0, unroll=5)
-    receive(3, m2, 0, 1)
-    electric_second(0, 0)
-    outs = [
-        pltpu.make_async_copy(efin, e_out, out_sem.at[0]),
-        pltpu.make_async_copy(afin, a_out, out_sem.at[1]),
-    ]
-    for c in outs:
-        c.start()
+    receive(3, 0, m2, 1, 3)
+    lax.fori_loop(1, 16, drive_second, 0, unroll=5)
+    receive(3, 0, m2, 0, 1)
+    drive_second(0, 0)
     for c in bases:
         c.wait()
 
@@ -454,7 +460,7 @@
         partial[pl.ds(start, 16), :] = jnp.where(row % 2 == 0, acc[:, :128], acc[:, 128:])
         return 0
 
-    lax.fori_loop(0, 8, tiles, 0, unroll=2)
+    lax.fori_loop(0, 8, tiles, 0, unroll=4)
 
     part = partial[...]
     turned = pltpu.roll(part, 64, 1)
@@ -473,8 +479,29 @@
     slots = slots + lax.dot_general(place[...], lo, (((1,), (0,)), ((), ())), preferred_element_type=F32)
     for p in range(2):
         vsend[pl.ds(p, PLANES, stride=3), 0, :] = slots[p * PLANES : (p + 1) * PLANES]
-    pl.semaphore_wait(ready_sem, 15)
+    pl.semaphore_wait(ready_sem.at[1], 3)
     spread()
+
+    def fields(y, _):
+        rat, sil = ratio[y], silver[y]
+        back = minus_turn(3, 1, m2, y)
+        for c in "xyz":
+            new = p2[IDX[(c, 0)], y] + rat * efin[COMP[c], y]
+            if c == "z":
+                new = new + source_level * source_wave[1] * sources[y]
+            efin[COMP[c], y] = new
+            adj_drive = -drude_keep * (sil * p1[IDX[(c, 1)], y]) - p2[IDX[(c, 1)], y]
+            afin[COMP[c], y] = adj1[COMP[c], y] + drude_gain * (sil * adj_drive) - time_step * back[c]
+        return 0
+
+    receive(3, 1, m2, 0, 3)
+    lax.fori_loop(0, 16, fields, 0, unroll=4)
+    outs = [
+        pltpu.make_async_copy(efin, e_out, out_sem.at[0]),
+        pltpu.make_async_copy(afin, a_out, out_sem.at[1]),
+    ]
+    for c in outs:
+        c.start()
 
     gathered()
     ids = vrecv[pl.ds(2, PLANES, stride=3), 0, :]
@@ -498,7 +525,8 @@
     for c in outs:
         c.wait()
     for r, field in enumerate((p1, m1, p2, m2)):
-        sent(r, field)
+        for t in range(2):
+            sent(r, t, field)
     all_sent()
     last.wait()
 
@@ -544,6 +572,7 @@
             V(brick, F32),
             V(brick, F32),
             V(field, F32),
+            V(field, F32),
             V(brick, F32),
             V((256, 128), F32),
             V(field, F32),
@@ -551,10 +580,10 @@
             V((NB * KB, TILE), BF16),
             V((1, NB), jnp.int32),
             V((1, NB), jnp.int32),
-            V((4, 4, 16, 128), F32),
-            V((4, 4, 16, 128), F32),
-            V((4, 16, 128), F32),
-            V((4, 16, 128), F32),
+            V((4, 2, 2, 16, 128), F32),
+            V((4, 2, 2, 16, 128), F32),
+            V((4, 2, 16, 128), F32),
+            V((4, 2, 16, 128), F32),
             V((NB, 4 * TILES), BF16),
             V((TILES, 128), F32),
             V((3 * PLANES, 1, 128), F32),
@@ -563,11 +592,11 @@
             D((10,)),
             D((NCHUNK,)),
             D((3,)),
-            D((4, 3)),
-            D((4, 3)),
+            D((8, 3)),
+            D((8, 3)),
             D((2,)),
             D,
-            pltpu.SemaphoreType.REGULAR,
+            pltpu.SemaphoreType.REGULAR((2,)),
         ],
         compiler_params=pltpu.CompilerParams(
             collective_id=0, has_side_effects=True, vmem_limit_bytes=56000 << 10

time: 43.7 us -> 42.3 us (0.968)
  Pallas kernels: 37.9 us -> 36.5 us
    pallas_call x1, Pallas kernels: 37.9 us -> 36.5 us  [local(): pl.pallas_call(kernel, name='adjoint_step', out_shape=(jax.ShapeDtypeStru...]
where the time goes in v5:
time: 42.3 us; the launch traced here: 42.1 us
  Pallas kernels  36.5 us (86%)
  local copies, waits for them, and re-layouts  4.91 us (12%)
  between operations  0.64 us (2%)
    pallas_call x1, Pallas kernels, local(): pl.pallas_call(kernel, name='adjoint_step', out_shape=(jax.ShapeDtypeStru...  36.5 us
    unnamed x3, local copies, waits for them, and re-layouts  4.91 us

profile of v5, /device:TPU:8, one launch (start us, length us, event | category | flops | bytes accessed | tf_op | source)
XLA Modules:
  0.0 42.1 jit_solution(15827836278974981057)
XLA Ops:
  0.6 36.5 %adjoint_step.1 = (f32[3,16,16,128]{3,2,1,0:T(8,128)}, f32[3,16,16,128]{3,2,1,0:T(8,128)}, f32[64,128]{1,0:T(8,128)}) custom-call(s32[8]{0:T(128)} %source_ref.1, f32[3,16,16,128]{3,2,1,0:T(8,128)} %e0_hbm.1, f32[3,16,16,128]{3,2,1,0:T(8,128)} %h0_hbm.1, f32[3,16,16,128]{3,2,1,0:T(8,128)} %j0_hbm.1, f32[3,16,16,128]{3,2,1,0:T(8,128)} %cot_hbm.1, ...), custom_call_target="tpu_custom_call" | custom-call | tf_op jit(solution)/shard_map/adjoint_step/pallas_call | solution.py:550
  37.2 1.8 %copy.16 = f32[3,16,16,128]{3,2,1,0:T(8,128)} copy(f32[3,16,16,128]{3,2,1,0:T(8,128)} %get-tuple-element.6) | data formatting | bytes 786432
  38.9 1.8 %copy.17 = f32[3,16,16,128]{3,2,1,0:T(8,128)} copy(f32[3,16,16,128]{3,2,1,0:T(8,128)} %get-tuple-element.7) | data formatting | bytes 786432
  40.7 1.4 %copy.18 = f32[64,128]{1,0:T(8,128)} copy(f32[64,128]{1,0:T(8,128)} %get-tuple-element.8) | data formatting | bytes 65536

commit v6 on v5

--- a/solution.py
+++ b/solution.py
@@ -72,8 +72,6 @@
     drive1,
     part1,
     grad,
-    efin,
-    afin,
     basis,
     owner,
     group,
@@ -85,10 +83,8 @@
     partial,
     vsend,
     vrecv,
-    coef,
     in_sem,
     basis_sem,
-    out_sem,
     send_sem,
     recv_sem,
     a2a_sem,
@@ -432,7 +428,7 @@
         for c in "xyz":
             cur = sil * (drude_keep * j0[COMP[c], y] + drude_gain * p2[IDX[(c, 0)], y])
             drive = turn[c] - cur
-            efin[COMP[c], y] = drive
+            e_out[COMP[c], y] = drive
             total = total + p1[IDX[(c, 1)], y] * drive
         grad[pl.ds(pl.multiple_of(y * 16, 16), 16), :] = factor[y] * total
         return 0
@@ -486,22 +482,16 @@
         rat, sil = ratio[y], silver[y]
         back = minus_turn(3, 1, m2, y)
         for c in "xyz":
-            new = p2[IDX[(c, 0)], y] + rat * efin[COMP[c], y]
+            new = p2[IDX[(c, 0)], y] + rat * e_out[COMP[c], y]
             if c == "z":
                 new = new + source_level * source_wave[1] * sources[y]
-            efin[COMP[c], y] = new
+            e_out[COMP[c], y] = new
             adj_drive = -drude_keep * (sil * p1[IDX[(c, 1)], y]) - p2[IDX[(c, 1)], y]
-            afin[COMP[c], y] = adj1[COMP[c], y] + drude_gain * (sil * adj_drive) - time_step * back[c]
+            a_out[COMP[c], y] = adj1[COMP[c], y] + drude_gain * (sil * adj_drive) - time_step * back[c]
         return 0
 
     receive(3, 1, m2, 0, 3)
     lax.fori_loop(0, 16, fields, 0, unroll=4)
-    outs = [
-        pltpu.make_async_copy(efin, e_out, out_sem.at[0]),
-        pltpu.make_async_copy(afin, a_out, out_sem.at[1]),
-    ]
-    for c in outs:
-        c.start()
 
     gathered()
     ids = vrecv[pl.ds(2, PLANES, stride=3), 0, :]
@@ -519,16 +509,11 @@
     hi, lo = split(vals)
     both = lax.dot_general(hi, hits, (((0,), (0,)), ((), ())), preferred_element_type=F32)
     both = both + lax.dot_general(lo, hits, (((0,), (0,)), ((), ())), preferred_element_type=F32)
-    coef[...] = both[:KB, :GRP_DEV] + both[KB:, GRP_DEV:]
-    last = pltpu.make_async_copy(coef, coef_out, out_sem.at[2])
-    last.start()
-    for c in outs:
-        c.wait()
+    coef_out[...] = both[:KB, :GRP_DEV] + both[KB:, GRP_DEV:]
     for r, field in enumerate((p1, m1, p2, m2)):
         for t in range(2):
             sent(r, t, field)
     all_sent()
-    last.wait()
 
 
 def local(
@@ -551,12 +536,12 @@
         kernel,
         name="adjoint_step",
         out_shape=(
-            jax.ShapeDtypeStruct(field, F32),
-            jax.ShapeDtypeStruct(field, F32),
-            jax.ShapeDtypeStruct((KB, GRP_DEV), F32),
+            V(field, F32),
+            V(field, F32),
+            V((KB, GRP_DEV), F32),
         ),
         in_specs=[pl.BlockSpec(memory_space=pltpu.SMEM)] + [anywhere] * 9,
-        out_specs=(anywhere,) * 3,
+        out_specs=(pl.BlockSpec(memory_space=pltpu.VMEM),) * 3,
         scratch_shapes=[
             V((6, 17, 16, 128), F32),
             V((6, 17, 16, 128), F32),
@@ -575,8 +560,6 @@
             V(field, F32),
             V(brick, F32),
             V((256, 128), F32),
-            V(field, F32),
-            V(field, F32),
             V((NB * KB, TILE), BF16),
             V((1, NB), jnp.int32),
             V((1, NB), jnp.int32),
@@ -588,10 +571,8 @@
             V((TILES, 128), F32),
             V((3 * PLANES, 1, 128), F32),
             V((3 * PLANES, 1, 128), F32),
-            V((KB, GRP_DEV), F32),
             D((10,)),
             D((NCHUNK,)),
-            D((3,)),
             D((8, 3)),
             D((8, 3)),
             D((2,)),

time: 42.3 us -> 38.8 us (0.917)
  local copies, waits for them, and re-layouts: 4.91 us -> 2.11 us
  Pallas kernels: 36.5 us -> 35.9 us
    unnamed x3, local copies, waits for them, and re-layouts: 4.91 us -> 2.11 us
    pallas_call x1, Pallas kernels: 36.5 us -> 35.9 us  [local(): pl.pallas_call(kernel, name='adjoint_step', out_shape=(V(field, F32), V(f...]
where the time goes in v6:
time: 38.8 us; the launch traced here: 38.7 us
  Pallas kernels  35.9 us (93%)
  local copies, waits for them, and re-layouts  2.11 us (5%)
  between operations  0.64 us (2%)
    pallas_call x1, Pallas kernels, local(): pl.pallas_call(kernel, name='adjoint_step', out_shape=(V(field, F32), V(f...  35.9 us
    unnamed x3, local copies, waits for them, and re-layouts  2.11 us

profile of v6, /device:TPU:8, one launch (start us, length us, event | category | flops | bytes accessed | tf_op | source)
XLA Modules:
  0.0 38.7 jit_solution(4609057804495567089)
XLA Ops:
  0.6 35.9 %adjoint_step.1 = (f32[3,16,16,128]{3,2,1,0:T(8,128)S(1)}, f32[3,16,16,128]{3,2,1,0:T(8,128)S(1)}, f32[64,128]{1,0:T(8,128)S(1)}) custom-call(s32[8]{0:T(128)} %source_ref.1, f32[3,16,16,128]{3,2,1,0:T(8,128)} %e0_hbm.1, f32[3,16,16,128]{3,2,1,0:T(8,128)} %h0_hbm.1, f32[3,16,16,128]{3,2,1,0:T(8,128)} %j0_hbm.1, f32[3,16,16,128]{3,2,1,0:T(8,128)} %cot_hbm.1, ...), custom_call_target="tpu_custom_call" | custom-call | tf_op jit(solution)/shard_map/adjoint_step/pallas_call | solution.py:535
  36.6 0.7 %copy.16 = f32[3,16,16,128]{3,2,1,0:T(8,128)} copy(f32[3,16,16,128]{3,2,1,0:T(8,128)S(1)} %get-tuple-element.3) | data formatting | bytes 786432
  37.3 0.6 %copy.18 = f32[64,128]{1,0:T(8,128)} copy(f32[64,128]{1,0:T(8,128)S(1)} %get-tuple-element.5) | data formatting | bytes 65536
  37.9 0.7 %copy.17 = f32[3,16,16,128]{3,2,1,0:T(8,128)} copy(f32[3,16,16,128]{3,2,1,0:T(8,128)S(1)} %get-tuple-element.4) | data formatting | bytes 786432

commit v7 on v6

--- a/solution.py
+++ b/solution.py
@@ -516,6 +516,15 @@
     all_sent()
 
 
+def deliver(e_ref, a_ref, coef_ref, e_out, a_out, coef_out, sem):
+    pairs = ((e_ref, e_out), (a_ref, a_out), (coef_ref, coef_out))
+    copies = [pltpu.make_async_copy(s, d, sem.at[i]) for i, (s, d) in enumerate(pairs)]
+    for c in copies:
+        c.start()
+    for c in copies:
+        c.wait()
+
+
 def local(
     electric_start,
     magnetic_start,
@@ -532,7 +541,7 @@
     brick = (16, 16, 128)
     anywhere = pl.BlockSpec(memory_space=pltpu.HBM)
     V, D = pltpu.VMEM, pltpu.SemaphoreType.DMA
-    return pl.pallas_call(
+    results = pl.pallas_call(
         kernel,
         name="adjoint_step",
         out_shape=(
@@ -594,6 +603,19 @@
         block_owner.reshape(1, NB),
         block_group.reshape(1, NB),
     )
+    return pl.pallas_call(
+        deliver,
+        name="deliver",
+        out_shape=(
+            jax.ShapeDtypeStruct(field, F32),
+            jax.ShapeDtypeStruct(field, F32),
+            jax.ShapeDtypeStruct((KB, GRP_DEV), F32),
+        ),
+        in_specs=[pl.BlockSpec(memory_space=pltpu.VMEM)] * 3,
+        out_specs=(anywhere,) * 3,
+        scratch_shapes=[D((3,))],
+        compiler_params=pltpu.CompilerParams(vmem_limit_bytes=2 << 20),
+    )(*(pltpu.with_memory_space_constraint(x, pltpu.VMEM) for x in results))
 
 
 def solution(mesh):

time: 38.8 us -> 37.6 us (0.969)
  local copies, waits for them, and re-layouts: 2.11 us -> 0 us
  Pallas kernels: 35.9 us -> 36.8 us
    unnamed x3 -> x0, local copies, waits for them, and re-layouts: 2.11 us -> none
    pallas_call x0 -> x1, Pallas kernels: none -> 0.91 us  [local(): pl.pallas_call(deliver, name='deliver', out_shape=(jax.ShapeDtypeStruct(f...]
where the time goes in v7:
time: 37.6 us; the launch traced here: 37.5 us
  Pallas kernels  36.8 us (98%)
  between operations  0.64 us (2%)
    pallas_call x1, Pallas kernels, local(): pl.pallas_call(kernel, name='adjoint_step', out_shape=(V(field, F32), V(f...  35.9 us
    pallas_call x1, Pallas kernels, local(): pl.pallas_call(deliver, name='deliver', out_shape=(jax.ShapeDtypeStruct(f...  0.91 us

profile of v7, /device:TPU:8, one launch (start us, length us, event | category | flops | bytes accessed | tf_op | source)
XLA Modules:
  0.0 37.5 jit_solution(11091664645423134788)
XLA Ops:
  0.6 35.9 %adjoint_step.1 = (f32[3,16,16,128]{3,2,1,0:T(8,128)S(1)}, f32[3,16,16,128]{3,2,1,0:T(8,128)S(1)}, f32[64,128]{1,0:T(8,128)S(1)}) custom-call(s32[8]{0:T(128)} %source_ref.1, f32[3,16,16,128]{3,2,1,0:T(8,128)} %e0_hbm.1, f32[3,16,16,128]{3,2,1,0:T(8,128)} %h0_hbm.1, f32[3,16,16,128]{3,2,1,0:T(8,128)} %j0_hbm.1, f32[3,16,16,128]{3,2,1,0:T(8,128)} %cot_hbm.1, ...), custom_call_target="tpu_custom_call" | custom-call | tf_op jit(solution)/shard_map/adjoint_step/pallas_call | solution.py:544
  36.6 0.9 %deliver.1 = (f32[3,16,16,128]{3,2,1,0:T(8,128)}, f32[3,16,16,128]{3,2,1,0:T(8,128)}, f32[64,128]{1,0:T(8,128)}) custom-call(f32[3,16,16,128]{3,2,1,0:T(8,128)S(1)} %get-tuple-element.6.e_ref, f32[3,16,16,128]{3,2,1,0:T(8,128)S(1)} %get-tuple-element.7.a_ref, f32[64,128]{1,0:T(8,128)S(1)} %get-tuple-element.8.coef_ref), custom_call_target="tpu_custom_call" | custom-call | tf_op jit(solution)/shard_map/deliver/pallas_call | solution.py:606

commit v8 on v7

--- a/solution.py
+++ b/solution.py
@@ -456,7 +456,7 @@
         partial[pl.ds(start, 16), :] = jnp.where(row % 2 == 0, acc[:, :128], acc[:, 128:])
         return 0
 
-    lax.fori_loop(0, 8, tiles, 0, unroll=4)
+    lax.fori_loop(0, 8, tiles, 0, unroll=8)
 
     part = partial[...]
     turned = pltpu.roll(part, 64, 1)
@@ -470,9 +470,9 @@
         ],
         axis=0,
     )
-    hi, lo = split(stack)
-    slots = lax.dot_general(place[...], hi, (((1,), (0,)), ((), ())), preferred_element_type=F32)
-    slots = slots + lax.dot_general(place[...], lo, (((1,), (0,)), ((), ())), preferred_element_type=F32)
+    halves = jnp.concatenate(split(stack), axis=1)
+    slots = lax.dot_general(place[...], halves, (((1,), (0,)), ((), ())), preferred_element_type=F32)
+    slots = slots[:, :128] + slots[:, 128:]
     for p in range(2):
         vsend[pl.ds(p, PLANES, stride=3), 0, :] = slots[p * PLANES : (p + 1) * PLANES]
     pl.semaphore_wait(ready_sem.at[1], 3)

time: 37.6 us -> 37.4 us (level)
  no operation moved by 1% of the time
where the time goes in v8:
time: 37.4 us; the launch traced here: 37.3 us
  Pallas kernels  36.6 us (98%)
  between operations  0.64 us (2%)
    pallas_call x1, Pallas kernels, local(): pl.pallas_call(kernel, name='adjoint_step', out_shape=(V(field, F32), V(f...  35.7 us
    pallas_call x1, Pallas kernels, local(): pl.pallas_call(deliver, name='deliver', out_shape=(jax.ShapeDtypeStruct(f...  0.91 us

profile of v8, /device:TPU:8, one launch (start us, length us, event | category | flops | bytes accessed | tf_op | source)
XLA Modules:
  0.0 37.3 jit_solution(3215005651837481627)
XLA Ops:
  0.6 35.7 %adjoint_step.1 = (f32[3,16,16,128]{3,2,1,0:T(8,128)S(1)}, f32[3,16,16,128]{3,2,1,0:T(8,128)S(1)}, f32[64,128]{1,0:T(8,128)S(1)}) custom-call(s32[8]{0:T(128)} %source_ref.1, f32[3,16,16,128]{3,2,1,0:T(8,128)} %e0_hbm.1, f32[3,16,16,128]{3,2,1,0:T(8,128)} %h0_hbm.1, f32[3,16,16,128]{3,2,1,0:T(8,128)} %j0_hbm.1, f32[3,16,16,128]{3,2,1,0:T(8,128)} %cot_hbm.1, ...), custom_call_target="tpu_custom_call" | custom-call | tf_op jit(solution)/shard_map/adjoint_step/pallas_call | solution.py:544
  36.4 0.9 %deliver.1 = (f32[3,16,16,128]{3,2,1,0:T(8,128)}, f32[3,16,16,128]{3,2,1,0:T(8,128)}, f32[64,128]{1,0:T(8,128)}) custom-call(f32[3,16,16,128]{3,2,1,0:T(8,128)S(1)} %get-tuple-element.6.e_ref, f32[3,16,16,128]{3,2,1,0:T(8,128)S(1)} %get-tuple-element.7.a_ref, f32[64,128]{1,0:T(8,128)S(1)} %get-tuple-element.8.coef_ref), custom_call_target="tpu_custom_call" | custom-call | tf_op jit(solution)/shard_map/deliver/pallas_call | solution.py:606
